TPU v7x, 128 devices: a whole 4x4x4 slice. The times are simulated.
128 devices in a mesh: layer: 16 (over y, z), batch: 8 (over x, core).
Axes of the slice: x: 4, y: 4, z: 4, core: 2. Of those that a mesh axis runs over, the one named last changes fastest.
Arguments:
- inputs: bfloat16 [1024, 4096], P('batch'), may hold values from -6 to 6
- warm_states: bfloat16 [16, 1024, 4096], P('layer', 'batch'), may hold values from -24 to 24
- weights: bfloat16 [64, 32, 4, 128, 128], P('layer'), may hold values from -0.25 to 0.25
- pattern: int32 [64, 32, 4], P('layer'), may hold values from 0 to 31, as said below
- bias: float32 [64, 4096], P('layer'), may hold values from -3 to 3
Outputs:
- ends: bfloat16 [16, 1024, 4096], P('layer', 'batch')
- norms: float32 [2], replicated
Inputs may be any that keep to these rules, and one draw needn't show every extreme that they name: `pattern`: for every layer and output block column, the 4 entries are different block indices.
All inputs are finite; a program needn't handle non-finite values.
Results may differ from a plain program's by a relative error of at most 0.04.
Values may be sent and summed in bfloat16 or wider, within the bound.
A program may use at most 128 MiB of HBM per device.

v0:
```python
import jax
import jax.numpy as jnp
from jax import lax
from jax.sharding import PartitionSpec as P

ITERS = 2


STEP = 0.25


def passed_along(value, axis, steps):
    count = lax.axis_size(axis)
    leading, last = (max(0, -steps), min(count, count - steps))
    return lax.ppermute(value, axis, [(source, source + steps) for source in range(leading, last)])


def preact(state, weight, pattern, bias):
    rows = state.shape[0]
    nblk, kblk, size = (weight.shape[0], weight.shape[1], weight.shape[2])
    blocks = state.reshape(rows, nblk, size)
    picked = jnp.take(blocks, pattern.reshape(-1), axis=1).reshape(rows, nblk, kblk, size)
    out = jnp.einsum("rnki,nkio->rno", picked, weight, preferred_element_type=jnp.float32)
    return out.reshape(rows, nblk * size) + bias


def fine_step(state, weight, pattern, bias):
    return (
        state.astype(jnp.float32) + STEP * jnp.tanh(preact(state, weight, pattern, bias))
    ).astype(jnp.bfloat16)


def coarse_step(state, weight, pattern, bias, factor):
    return state.astype(jnp.float32) + factor * STEP * jnp.tanh(
        preact(state, weight, pattern, bias)
    )


def on_device(inputs, warm_states, weights, pattern, bias):
    layers_dev = weights.shape[0]
    chain_len = lax.axis_size("layer")
    index = lax.axis_index("layer")
    ends = warm_states[0]
    row_count = ends.shape[0]
    count = float(chain_len * lax.axis_size("batch") * row_count * ends.shape[1])
    norms = []
    for outer in range(ITERS):
        moved = passed_along(ends, "layer", 1)
        start = jnp.where(index == 0, inputs, moved)
        state = start
        for layer in range(layers_dev):
            state = fine_step(state, weights[layer], pattern[layer], bias[layer])
        diff = state.astype(jnp.float32) - ends.astype(jnp.float32)
        total = lax.psum(jnp.sum(diff * diff), ("layer", "batch"))
        norms.append(jnp.sqrt(total / count))
        tau = state.astype(jnp.float32) - coarse_step(
            start, weights[0], pattern[0], bias[0], layers_dev
        )

        def turn(step, carry):
            incoming, result = carry
            source = jnp.where(index == 0, inputs, incoming)
            value = (coarse_step(source, weights[0], pattern[0], bias[0], layers_dev) + tau).astype(
                jnp.bfloat16
            )
            result = jnp.where(index == step, value, result)
            incoming = passed_along(value, "layer", 1)
            return (incoming, result)

        _, ends = lax.fori_loop(0, chain_len, turn, (jnp.zeros_like(ends), ends))
    return (ends[None], jnp.stack(norms))


def solution(mesh):
    in_specs = (
        P("batch", None),
        P("layer", "batch", None),
        P("layer", None, None, None, None),
        P("layer", None, None),
        P("layer", None),
    )
    out_specs = (P("layer", "batch", None), P())
    return jax.shard_map(
        on_device, mesh=mesh, in_specs=in_specs, out_specs=out_specs, check_vma=False
    )
```

profile of v0, /device:TPU:0, one launch (start us, length us, event | category | flops | bytes accessed | tf_op | source)
XLA Modules:
  0.0 1345.3 jit_solution(18401446180854897489)
XLA Ops:
  3.0 4.0 collective-permute-start.2
  11.6 21.2 %copy.53 = bf16[4,32,4,128,128]{3,4,2,1,0:T(8,128)(2,1)} copy(bf16[4,32,4,128,128]{4,3,2,1,0:T(8,128)(2,1)} %param.13) | data formatting | bytes 33554432 | tf_op jit(solution)/shard_map/while | solution.py:70
  40.0 3.5 fusion.14
  51.4 3.5 fusion.16
  61.5 3.5 fusion.18
  79.9 561.8 %while.32 = (s32[]{:T(128)}, bf16[128,4096]{0,1:T(8,128)(2,1)S(1)}, bf16[128,4096]{0,1:T(8,128)(2,1)}, pred[]{:T(512)}, bf16[128,4096]{0,1:T(8,128)(2,1)}, /*ind...) while((s32[]{:T(128)}, bf16[128,4096]{0,1:T(8,128)(2,1)S(1)}, ...), condition=%wide.region_1.3_spmd, body=%wide.region_0.2_spmd.sunk | while | flops 542640256 | bytes 43049888 | solution.py:70
  95.5 22.4 %collective-permute-done = bf16[128,4096]{0,1:T(8,128)(2,1)S(1)} collective-permute-done((bf16[128,4096]{0,1:T(8,128)(2,1)}, bf16[128,4096]{0,1:T(8,128)(2,1)S(1)}, u32[]{:S(2)}, u32[]{:S(2)}) %collective-permute-start) | collective-permute-done | bytes 1048608 | tf_op jit(solution)/shard_map/while/body/eval_jaxpr/ppermute | solution.py:15
  134.8 21.5 %collective-permute-done = bf16[128,4096]{0,1:T(8,128)(2,1)S(1)} collective-permute-done((bf16[128,4096]{0,1:T(8,128)(2,1)}, bf16[128,4096]{0,1:T(8,128)(2,1)S(1)}, u32[]{:S(2)}, u32[]{:S(2)}) %collective-permute-start) | collective-permute-done | bytes 1048608 | tf_op jit(solution)/shard_map/while/body/eval_jaxpr/ppermute | solution.py:15
  173.5 20.5 %collective-permute-done = bf16[128,4096]{0,1:T(8,128)(2,1)S(1)} collective-permute-done((bf16[128,4096]{0,1:T(8,128)(2,1)}, bf16[128,4096]{0,1:T(8,128)(2,1)S(1)}, u32[]{:S(2)}, u32[]{:S(2)}) %collective-permute-start) | collective-permute-done | bytes 1048608 | tf_op jit(solution)/shard_map/while/body/eval_jaxpr/ppermute | solution.py:15
  211.2 19.6 %collective-permute-done = bf16[128,4096]{0,1:T(8,128)(2,1)S(1)} collective-permute-done((bf16[128,4096]{0,1:T(8,128)(2,1)}, bf16[128,4096]{0,1:T(8,128)(2,1)S(1)}, u32[]{:S(2)}, u32[]{:S(2)}) %collective-permute-start) | collective-permute-done | bytes 1048608 | tf_op jit(solution)/shard_map/while/body/eval_jaxpr/ppermute | solution.py:15
  248.0 18.7 %collective-permute-done = bf16[128,4096]{0,1:T(8,128)(2,1)S(1)} collective-permute-done((bf16[128,4096]{0,1:T(8,128)(2,1)}, bf16[128,4096]{0,1:T(8,128)(2,1)S(1)}, u32[]{:S(2)}, u32[]{:S(2)}) %collective-permute-start) | collective-permute-done | bytes 1048608 | tf_op jit(solution)/shard_map/while/body/eval_jaxpr/ppermute | solution.py:15
  280.7 3.9 collective-permute-start
  284.7 17.8 %collective-permute-done = bf16[128,4096]{0,1:T(8,128)(2,1)S(1)} collective-permute-done((bf16[128,4096]{0,1:T(8,128)(2,1)}, bf16[128,4096]{0,1:T(8,128)(2,1)S(1)}, u32[]{:S(2)}, u32[]{:S(2)}) %collective-permute-start) | collective-permute-done | bytes 1048608 | tf_op jit(solution)/shard_map/while/body/eval_jaxpr/ppermute | solution.py:15
  316.5 5.5 collective-permute-start
  322.0 16.8 %collective-permute-done = bf16[128,4096]{0,1:T(8,128)(2,1)S(1)} collective-permute-done((bf16[128,4096]{0,1:T(8,128)(2,1)}, bf16[128,4096]{0,1:T(8,128)(2,1)S(1)}, u32[]{:S(2)}, u32[]{:S(2)}) %collective-permute-start) | collective-permute-done | bytes 1048608 | tf_op jit(solution)/shard_map/while/body/eval_jaxpr/ppermute | solution.py:15
  352.9 5.0 collective-permute-start
  357.9 15.9 %collective-permute-done = bf16[128,4096]{0,1:T(8,128)(2,1)S(1)} collective-permute-done((bf16[128,4096]{0,1:T(8,128)(2,1)}, bf16[128,4096]{0,1:T(8,128)(2,1)S(1)}, u32[]{:S(2)}, u32[]{:S(2)}) %collective-permute-start) | collective-permute-done | bytes 1048608 | tf_op jit(solution)/shard_map/while/body/eval_jaxpr/ppermute | solution.py:15
  387.8 5.2 collective-permute-start
  393.1 15.0 %collective-permute-done = bf16[128,4096]{0,1:T(8,128)(2,1)S(1)} collective-permute-done((bf16[128,4096]{0,1:T(8,128)(2,1)}, bf16[128,4096]{0,1:T(8,128)(2,1)S(1)}, u32[]{:S(2)}, u32[]{:S(2)}) %collective-permute-start) | collective-permute-done | bytes 1048608 | tf_op jit(solution)/shard_map/while/body/eval_jaxpr/ppermute | solution.py:15
  422.1 5.2 collective-permute-start
  427.4 14.1 %collective-permute-done = bf16[128,4096]{0,1:T(8,128)(2,1)S(1)} collective-permute-done((bf16[128,4096]{0,1:T(8,128)(2,1)}, bf16[128,4096]{0,1:T(8,128)(2,1)S(1)}, u32[]{:S(2)}, u32[]{:S(2)}) %collective-permute-start) | collective-permute-done | bytes 1048608 | tf_op jit(solution)/shard_map/while/body/eval_jaxpr/ppermute | solution.py:15
  455.5 5.2 collective-permute-start
  460.7 13.2 collective-permute-done
  488.0 5.2 collective-permute-start
  493.2 12.5 collective-permute-done
  519.8 5.2 collective-permute-start
  525.0 12.5 collective-permute-done
  551.6 5.2 collective-permute-start
  556.9 12.5 collective-permute-done
  583.5 5.2 collective-permute-start
  588.7 12.5 collective-permute-done
  615.3 5.2 collective-permute-start
  620.5 21.1 %collective-permute-done = bf16[128,4096]{0,1:T(8,128)(2,1)S(1)} collective-permute-done((bf16[128,4096]{0,1:T(8,128)(2,1)}, bf16[128,4096]{0,1:T(8,128)(2,1)S(1)}, u32[]{:S(2)}, u32[]{:S(2)}) %collective-permute-start) | collective-permute-done | bytes 1048608 | tf_op jit(solution)/shard_map/while/body/eval_jaxpr/ppermute | solution.py:15
  641.7 6.7 collective-permute-start.3
  648.4 12.5 collective-permute-done.3
  705.7 77.2 %all-reduce = (f32[]{:T(128)}, f32[]{:T(128)}) all-reduce(f32[]{:T(128)} %get-tuple-element.483, f32[]{:T(128)} %get-tuple-element.481), channel_id=1, replica_groups=mesh['layer'=16,'batch'=8] {'layer','batch'}, use_global_device_ids=true, to_apply=%region_7.9 | all-reduce | flops 2 | bytes 16 | tf_op jit(solution)/shard_map/psum | solution.py:54
  787.3 555.2 %while.33 = (s32[]{:T(128)}, bf16[128,4096]{0,1:T(8,128)(2,1)S(1)}, bf16[128,4096]{0,1:T(8,128)(2,1)}, pred[]{:T(512)}, bf16[128,4096]{0,1:T(8,128)(2,1)}, /*ind...) while((s32[]{:T(128)}, bf16[128,4096]{0,1:T(8,128)(2,1)S(1)}, ...), condition=%wide.region_3.5_spmd, body=%wide.region_2.4_spmd.sunk | while | flops 542640256 | bytes 43049888 | solution.py:70
  802.5 22.5 %collective-permute-done.1 = bf16[128,4096]{0,1:T(8,128)(2,1)S(1)} collective-permute-done((bf16[128,4096]{0,1:T(8,128)(2,1)}, bf16[128,4096]{0,1:T(8,128)(2,1)S(1)}, u32[]{:S(2)}, u32[]{:S(2)}) %collective-permute-start.1) | collective-permute-done | bytes 1048608 | tf_op jit(solution)/shard_map/while/body/eval_jaxpr/ppermute | solution.py:15
  841.9 21.6 %collective-permute-done.1 = bf16[128,4096]{0,1:T(8,128)(2,1)S(1)} collective-permute-done((bf16[128,4096]{0,1:T(8,128)(2,1)}, bf16[128,4096]{0,1:T(8,128)(2,1)S(1)}, u32[]{:S(2)}, u32[]{:S(2)}) %collective-permute-start.1) | collective-permute-done | bytes 1048608 | tf_op jit(solution)/shard_map/while/body/eval_jaxpr/ppermute | solution.py:15
  880.7 20.7 %collective-permute-done.1 = bf16[128,4096]{0,1:T(8,128)(2,1)S(1)} collective-permute-done((bf16[128,4096]{0,1:T(8,128)(2,1)}, bf16[128,4096]{0,1:T(8,128)(2,1)S(1)}, u32[]{:S(2)}, u32[]{:S(2)}) %collective-permute-start.1) | collective-permute-done | bytes 1048608 | tf_op jit(solution)/shard_map/while/body/eval_jaxpr/ppermute | solution.py:15
  918.5 19.7 %collective-permute-done.1 = bf16[128,4096]{0,1:T(8,128)(2,1)S(1)} collective-permute-done((bf16[128,4096]{0,1:T(8,128)(2,1)}, bf16[128,4096]{0,1:T(8,128)(2,1)S(1)}, u32[]{:S(2)}, u32[]{:S(2)}) %collective-permute-start.1) | collective-permute-done | bytes 1048608 | tf_op jit(solution)/shard_map/while/body/eval_jaxpr/ppermute | solution.py:15
  955.4 18.8 %collective-permute-done.1 = bf16[128,4096]{0,1:T(8,128)(2,1)S(1)} collective-permute-done((bf16[128,4096]{0,1:T(8,128)(2,1)}, bf16[128,4096]{0,1:T(8,128)(2,1)S(1)}, u32[]{:S(2)}, u32[]{:S(2)}) %collective-permute-start.1) | collective-permute-done | bytes 1048608 | tf_op jit(solution)/shard_map/while/body/eval_jaxpr/ppermute | solution.py:15
  988.3 4.1 collective-permute-start.1
  992.4 18.0 %collective-permute-done.1 = bf16[128,4096]{0,1:T(8,128)(2,1)S(1)} collective-permute-done((bf16[128,4096]{0,1:T(8,128)(2,1)}, bf16[128,4096]{0,1:T(8,128)(2,1)S(1)}, u32[]{:S(2)}, u32[]{:S(2)}) %collective-permute-start.1) | collective-permute-done | bytes 1048608 | tf_op jit(solution)/shard_map/while/body/eval_jaxpr/ppermute | solution.py:15
  1024.5 5.5 collective-permute-start.1
  1030.0 17.1 %collective-permute-done.1 = bf16[128,4096]{0,1:T(8,128)(2,1)S(1)} collective-permute-done((bf16[128,4096]{0,1:T(8,128)(2,1)}, bf16[128,4096]{0,1:T(8,128)(2,1)S(1)}, u32[]{:S(2)}, u32[]{:S(2)}) %collective-permute-start.1) | collective-permute-done | bytes 1048608 | tf_op jit(solution)/shard_map/while/body/eval_jaxpr/ppermute | solution.py:15
  1061.2 5.0 collective-permute-start.1
  1066.2 16.2 %collective-permute-done.1 = bf16[128,4096]{0,1:T(8,128)(2,1)S(1)} collective-permute-done((bf16[128,4096]{0,1:T(8,128)(2,1)}, bf16[128,4096]{0,1:T(8,128)(2,1)S(1)}, u32[]{:S(2)}, u32[]{:S(2)}) %collective-permute-start.1) | collective-permute-done | bytes 1048608 | tf_op jit(solution)/shard_map/while/body/eval_jaxpr/ppermute | solution.py:15
  1096.4 5.2 collective-permute-start.1
  1101.6 15.3 %collective-permute-done.1 = bf16[128,4096]{0,1:T(8,128)(2,1)S(1)} collective-permute-done((bf16[128,4096]{0,1:T(8,128)(2,1)}, bf16[128,4096]{0,1:T(8,128)(2,1)S(1)}, u32[]{:S(2)}, u32[]{:S(2)}) %collective-permute-start.1) | collective-permute-done | bytes 1048608 | tf_op jit(solution)/shard_map/while/body/eval_jaxpr/ppermute | solution.py:15
  1131.0 5.2 collective-permute-start.1
  1136.2 14.3 %collective-permute-done.1 = bf16[128,4096]{0,1:T(8,128)(2,1)S(1)} collective-permute-done((bf16[128,4096]{0,1:T(8,128)(2,1)}, bf16[128,4096]{0,1:T(8,128)(2,1)S(1)}, u32[]{:S(2)}, u32[]{:S(2)}) %collective-permute-start.1) | collective-permute-done | bytes 1048608 | tf_op jit(solution)/shard_map/while/body/eval_jaxpr/ppermute | solution.py:15
  1164.6 5.2 collective-permute-start.1
  1169.8 13.4 collective-permute-done.1
  1197.3 5.2 collective-permute-start.1
  1202.5 12.5 collective-permute-done.1
  1229.1 5.2 collective-permute-start.1
  1234.4 12.5 collective-permute-done.1
  1261.0 5.2 collective-permute-start.1
  1266.2 12.5 collective-permute-done.1
  1292.8 5.2 collective-permute-start.1
  1298.1 12.5 collective-permute-done.1
  1324.7 5.2 collective-permute-start.1
  1329.9 12.5 collective-permute-done.1
  (433 shorter events, 568.7 us)
Async XLA Ops:
  3.0 30.0 %collective-permute-start.2 = (bf16[128,4096]{0,1:T(8,128)(2,1)}, bf16[128,4096]{0,1:T(8,128)(2,1)S(1)}, u32[]{:S(2)}, u32[]{:S(2)}) collective-permute-start(bf16[128,4096]{0,1:T(8,128)(2,1)} %bitcast.18), channel_id=1, source_target_pairs={{0,8},{8,16},{16,24},{24,32},{32,40},{40,48},{48,56},{56,64},{64,7... | collective-permute-start | bytes 3145736 | tf_op jit(solution)/shard_map/ppermute | solution.py:15
  11.6 21.3 %copy-start.3 = (f32[4,4096]{1,0:T(4,128)S(1)}, f32[4,4096]{1,0:T(4,128)}, u32[]{:S(2)}) copy-start(f32[4,4096]{1,0:T(4,128)} %param.15) | copy-start | bytes 196612
  43.5 1.3 copy-start.1
  75.1 2.7 copy-start.2
  93.9 24.0 %collective-permute-start = (bf16[128,4096]{0,1:T(8,128)(2,1)}, bf16[128,4096]{0,1:T(8,128)(2,1)S(1)}, u32[]{:S(2)}, u32[]{:S(2)}) collective-permute-start(bf16[128,4096]{0,1:T(8,128)(2,1)} %get-tuple-element.609), channel_id=1, source_target_pairs={{0,8},{8,16},{16,24},{24,32},{32,40},{40,48},{48,56},{56,64},{64,7... | collective-permute-start | bytes 3145736 | tf_op jit(solution)/shard_map/while/body/eval_jaxpr/ppermute | solution.py:15
  131.9 24.3 %collective-permute-start = (bf16[128,4096]{0,1:T(8,128)(2,1)}, bf16[128,4096]{0,1:T(8,128)(2,1)S(1)}, u32[]{:S(2)}, u32[]{:S(2)}) collective-permute-start(bf16[128,4096]{0,1:T(8,128)(2,1)} %get-tuple-element.609), channel_id=1, source_target_pairs={{0,8},{8,16},{16,24},{24,32},{32,40},{40,48},{48,56},{56,64},{64,7... | collective-permute-start | bytes 3145736 | tf_op jit(solution)/shard_map/while/body/eval_jaxpr/ppermute | solution.py:15
  170.3 23.7 %collective-permute-start = (bf16[128,4096]{0,1:T(8,128)(2,1)}, bf16[128,4096]{0,1:T(8,128)(2,1)S(1)}, u32[]{:S(2)}, u32[]{:S(2)}) collective-permute-start(bf16[128,4096]{0,1:T(8,128)(2,1)} %get-tuple-element.609), channel_id=1, source_target_pairs={{0,8},{8,16},{16,24},{24,32},{32,40},{40,48},{48,56},{56,64},{64,7... | collective-permute-start | bytes 3145736 | tf_op jit(solution)/shard_map/while/body/eval_jaxpr/ppermute | solution.py:15
  208.1 22.7 %collective-permute-start = (bf16[128,4096]{0,1:T(8,128)(2,1)}, bf16[128,4096]{0,1:T(8,128)(2,1)S(1)}, u32[]{:S(2)}, u32[]{:S(2)}) collective-permute-start(bf16[128,4096]{0,1:T(8,128)(2,1)} %get-tuple-element.609), channel_id=1, source_target_pairs={{0,8},{8,16},{16,24},{24,32},{32,40},{40,48},{48,56},{56,64},{64,7... | collective-permute-start | bytes 3145736 | tf_op jit(solution)/shard_map/while/body/eval_jaxpr/ppermute | solution.py:15
  244.8 21.8 %collective-permute-start = (bf16[128,4096]{0,1:T(8,128)(2,1)}, bf16[128,4096]{0,1:T(8,128)(2,1)S(1)}, u32[]{:S(2)}, u32[]{:S(2)}) collective-permute-start(bf16[128,4096]{0,1:T(8,128)(2,1)} %get-tuple-element.609), channel_id=1, source_target_pairs={{0,8},{8,16},{16,24},{24,32},{32,40},{40,48},{48,56},{56,64},{64,7... | collective-permute-start | bytes 3145736 | tf_op jit(solution)/shard_map/while/body/eval_jaxpr/ppermute | solution.py:15
  280.7 21.7 %collective-permute-start = (bf16[128,4096]{0,1:T(8,128)(2,1)}, bf16[128,4096]{0,1:T(8,128)(2,1)S(1)}, u32[]{:S(2)}, u32[]{:S(2)}) collective-permute-start(bf16[128,4096]{0,1:T(8,128)(2,1)} %get-tuple-element.609), channel_id=1, source_target_pairs={{0,8},{8,16},{16,24},{24,32},{32,40},{40,48},{48,56},{56,64},{64,7... | collective-permute-start | bytes 3145736 | tf_op jit(solution)/shard_map/while/body/eval_jaxpr/ppermute | solution.py:15
  316.5 22.3 %collective-permute-start = (bf16[128,4096]{0,1:T(8,128)(2,1)}, bf16[128,4096]{0,1:T(8,128)(2,1)S(1)}, u32[]{:S(2)}, u32[]{:S(2)}) collective-permute-start(bf16[128,4096]{0,1:T(8,128)(2,1)} %get-tuple-element.609), channel_id=1, source_target_pairs={{0,8},{8,16},{16,24},{24,32},{32,40},{40,48},{48,56},{56,64},{64,7... | collective-permute-start | bytes 3145736 | tf_op jit(solution)/shard_map/while/body/eval_jaxpr/ppermute | solution.py:15
  352.9 20.9 %collective-permute-start = (bf16[128,4096]{0,1:T(8,128)(2,1)}, bf16[128,4096]{0,1:T(8,128)(2,1)S(1)}, u32[]{:S(2)}, u32[]{:S(2)}) collective-permute-start(bf16[128,4096]{0,1:T(8,128)(2,1)} %get-tuple-element.609), channel_id=1, source_target_pairs={{0,8},{8,16},{16,24},{24,32},{32,40},{40,48},{48,56},{56,64},{64,7... | collective-permute-start | bytes 3145736 | tf_op jit(solution)/shard_map/while/body/eval_jaxpr/ppermute | solution.py:15
  387.8 20.2 %collective-permute-start = (bf16[128,4096]{0,1:T(8,128)(2,1)}, bf16[128,4096]{0,1:T(8,128)(2,1)S(1)}, u32[]{:S(2)}, u32[]{:S(2)}) collective-permute-start(bf16[128,4096]{0,1:T(8,128)(2,1)} %get-tuple-element.609), channel_id=1, source_target_pairs={{0,8},{8,16},{16,24},{24,32},{32,40},{40,48},{48,56},{56,64},{64,7... | collective-permute-start | bytes 3145736 | tf_op jit(solution)/shard_map/while/body/eval_jaxpr/ppermute | solution.py:15
  422.1 19.3 %collective-permute-start = (bf16[128,4096]{0,1:T(8,128)(2,1)}, bf16[128,4096]{0,1:T(8,128)(2,1)S(1)}, u32[]{:S(2)}, u32[]{:S(2)}) collective-permute-start(bf16[128,4096]{0,1:T(8,128)(2,1)} %get-tuple-element.609), channel_id=1, source_target_pairs={{0,8},{8,16},{16,24},{24,32},{32,40},{40,48},{48,56},{56,64},{64,7... | collective-permute-start | bytes 3145736 | tf_op jit(solution)/shard_map/while/body/eval_jaxpr/ppermute | solution.py:15
  455.5 18.4 %collective-permute-start = (bf16[128,4096]{0,1:T(8,128)(2,1)}, bf16[128,4096]{0,1:T(8,128)(2,1)S(1)}, u32[]{:S(2)}, u32[]{:S(2)}) collective-permute-start(bf16[128,4096]{0,1:T(8,128)(2,1)} %get-tuple-element.609), channel_id=1, source_target_pairs={{0,8},{8,16},{16,24},{24,32},{32,40},{40,48},{48,56},{56,64},{64,7... | collective-permute-start | bytes 3145736 | tf_op jit(solution)/shard_map/while/body/eval_jaxpr/ppermute | solution.py:15
  488.0 17.8 %collective-permute-start = (bf16[128,4096]{0,1:T(8,128)(2,1)}, bf16[128,4096]{0,1:T(8,128)(2,1)S(1)}, u32[]{:S(2)}, u32[]{:S(2)}) collective-permute-start(bf16[128,4096]{0,1:T(8,128)(2,1)} %get-tuple-element.609), channel_id=1, source_target_pairs={{0,8},{8,16},{16,24},{24,32},{32,40},{40,48},{48,56},{56,64},{64,7... | collective-permute-start | bytes 3145736 | tf_op jit(solution)/shard_map/while/body/eval_jaxpr/ppermute | solution.py:15
  519.8 17.8 %collective-permute-start = (bf16[128,4096]{0,1:T(8,128)(2,1)}, bf16[128,4096]{0,1:T(8,128)(2,1)S(1)}, u32[]{:S(2)}, u32[]{:S(2)}) collective-permute-start(bf16[128,4096]{0,1:T(8,128)(2,1)} %get-tuple-element.609), channel_id=1, source_target_pairs={{0,8},{8,16},{16,24},{24,32},{32,40},{40,48},{48,56},{56,64},{64,7... | collective-permute-start | bytes 3145736 | tf_op jit(solution)/shard_map/while/body/eval_jaxpr/ppermute | solution.py:15
  551.6 17.8 %collective-permute-start = (bf16[128,4096]{0,1:T(8,128)(2,1)}, bf16[128,4096]{0,1:T(8,128)(2,1)S(1)}, u32[]{:S(2)}, u32[]{:S(2)}) collective-permute-start(bf16[128,4096]{0,1:T(8,128)(2,1)} %get-tuple-element.609), channel_id=1, source_target_pairs={{0,8},{8,16},{16,24},{24,32},{32,40},{40,48},{48,56},{56,64},{64,7... | collective-permute-start | bytes 3145736 | tf_op jit(solution)/shard_map/while/body/eval_jaxpr/ppermute | solution.py:15
  583.5 17.8 %collective-permute-start = (bf16[128,4096]{0,1:T(8,128)(2,1)}, bf16[128,4096]{0,1:T(8,128)(2,1)S(1)}, u32[]{:S(2)}, u32[]{:S(2)}) collective-permute-start(bf16[128,4096]{0,1:T(8,128)(2,1)} %get-tuple-element.609), channel_id=1, source_target_pairs={{0,8},{8,16},{16,24},{24,32},{32,40},{40,48},{48,56},{56,64},{64,7... | collective-permute-start | bytes 3145736 | tf_op jit(solution)/shard_map/while/body/eval_jaxpr/ppermute | solution.py:15
  615.3 26.4 %collective-permute-start = (bf16[128,4096]{0,1:T(8,128)(2,1)}, bf16[128,4096]{0,1:T(8,128)(2,1)S(1)}, u32[]{:S(2)}, u32[]{:S(2)}) collective-permute-start(bf16[128,4096]{0,1:T(8,128)(2,1)} %get-tuple-element.609), channel_id=1, source_target_pairs={{0,8},{8,16},{16,24},{24,32},{32,40},{40,48},{48,56},{56,64},{64,7... | collective-permute-start | bytes 3145736 | tf_op jit(solution)/shard_map/while/body/eval_jaxpr/ppermute | solution.py:15
  641.7 19.3 %collective-permute-start.3 = (bf16[128,4096]{0,1:T(8,128)(2,1)}, bf16[128,4096]{0,1:T(8,128)(2,1)S(1)}, u32[]{:S(2)}, u32[]{:S(2)}) collective-permute-start(bf16[128,4096]{0,1:T(8,128)(2,1)} %get-tuple-element.658), channel_id=1, source_target_pairs={{0,8},{8,16},{16,24},{24,32},{32,40},{40,48},{48,56},{56,64},{64,7... | collective-permute-start | bytes 3145736 | tf_op jit(solution)/shard_map/ppermute | solution.py:15
  671.5 1.4 copy-start
  801.1 23.8 %collective-permute-start.1 = (bf16[128,4096]{0,1:T(8,128)(2,1)}, bf16[128,4096]{0,1:T(8,128)(2,1)S(1)}, u32[]{:S(2)}, u32[]{:S(2)}) collective-permute-start(bf16[128,4096]{0,1:T(8,128)(2,1)} %get-tuple-element.621), channel_id=1, source_target_pairs={{0,8},{8,16},{16,24},{24,32},{32,40},{40,48},{48,56},{56,64},{64,7... | collective-permute-start | bytes 3145736 | tf_op jit(solution)/shard_map/while/body/eval_jaxpr/ppermute | solution.py:15
  839.0 24.5 %collective-permute-start.1 = (bf16[128,4096]{0,1:T(8,128)(2,1)}, bf16[128,4096]{0,1:T(8,128)(2,1)S(1)}, u32[]{:S(2)}, u32[]{:S(2)}) collective-permute-start(bf16[128,4096]{0,1:T(8,128)(2,1)} %get-tuple-element.621), channel_id=1, source_target_pairs={{0,8},{8,16},{16,24},{24,32},{32,40},{40,48},{48,56},{56,64},{64,7... | collective-permute-start | bytes 3145736 | tf_op jit(solution)/shard_map/while/body/eval_jaxpr/ppermute | solution.py:15
  877.5 23.8 %collective-permute-start.1 = (bf16[128,4096]{0,1:T(8,128)(2,1)}, bf16[128,4096]{0,1:T(8,128)(2,1)S(1)}, u32[]{:S(2)}, u32[]{:S(2)}) collective-permute-start(bf16[128,4096]{0,1:T(8,128)(2,1)} %get-tuple-element.621), channel_id=1, source_target_pairs={{0,8},{8,16},{16,24},{24,32},{32,40},{40,48},{48,56},{56,64},{64,7... | collective-permute-start | bytes 3145736 | tf_op jit(solution)/shard_map/while/body/eval_jaxpr/ppermute | solution.py:15
  915.4 22.9 %collective-permute-start.1 = (bf16[128,4096]{0,1:T(8,128)(2,1)}, bf16[128,4096]{0,1:T(8,128)(2,1)S(1)}, u32[]{:S(2)}, u32[]{:S(2)}) collective-permute-start(bf16[128,4096]{0,1:T(8,128)(2,1)} %get-tuple-element.621), channel_id=1, source_target_pairs={{0,8},{8,16},{16,24},{24,32},{32,40},{40,48},{48,56},{56,64},{64,7... | collective-permute-start | bytes 3145736 | tf_op jit(solution)/shard_map/while/body/eval_jaxpr/ppermute | solution.py:15
  952.3 22.0 %collective-permute-start.1 = (bf16[128,4096]{0,1:T(8,128)(2,1)}, bf16[128,4096]{0,1:T(8,128)(2,1)S(1)}, u32[]{:S(2)}, u32[]{:S(2)}) collective-permute-start(bf16[128,4096]{0,1:T(8,128)(2,1)} %get-tuple-element.621), channel_id=1, source_target_pairs={{0,8},{8,16},{16,24},{24,32},{32,40},{40,48},{48,56},{56,64},{64,7... | collective-permute-start | bytes 3145736 | tf_op jit(solution)/shard_map/while/body/eval_jaxpr/ppermute | solution.py:15
  988.3 22.1 %collective-permute-start.1 = (bf16[128,4096]{0,1:T(8,128)(2,1)}, bf16[128,4096]{0,1:T(8,128)(2,1)S(1)}, u32[]{:S(2)}, u32[]{:S(2)}) collective-permute-start(bf16[128,4096]{0,1:T(8,128)(2,1)} %get-tuple-element.621), channel_id=1, source_target_pairs={{0,8},{8,16},{16,24},{24,32},{32,40},{40,48},{48,56},{56,64},{64,7... | collective-permute-start | bytes 3145736 | tf_op jit(solution)/shard_map/while/body/eval_jaxpr/ppermute | solution.py:15
  1024.5 22.6 %collective-permute-start.1 = (bf16[128,4096]{0,1:T(8,128)(2,1)}, bf16[128,4096]{0,1:T(8,128)(2,1)S(1)}, u32[]{:S(2)}, u32[]{:S(2)}) collective-permute-start(bf16[128,4096]{0,1:T(8,128)(2,1)} %get-tuple-element.621), channel_id=1, source_target_pairs={{0,8},{8,16},{16,24},{24,32},{32,40},{40,48},{48,56},{56,64},{64,7... | collective-permute-start | bytes 3145736 | tf_op jit(solution)/shard_map/while/body/eval_jaxpr/ppermute | solution.py:15
  1061.2 21.2 %collective-permute-start.1 = (bf16[128,4096]{0,1:T(8,128)(2,1)}, bf16[128,4096]{0,1:T(8,128)(2,1)S(1)}, u32[]{:S(2)}, u32[]{:S(2)}) collective-permute-start(bf16[128,4096]{0,1:T(8,128)(2,1)} %get-tuple-element.621), channel_id=1, source_target_pairs={{0,8},{8,16},{16,24},{24,32},{32,40},{40,48},{48,56},{56,64},{64,7... | collective-permute-start | bytes 3145736 | tf_op jit(solution)/shard_map/while/body/eval_jaxpr/ppermute | solution.py:15
  1096.4 20.5 %collective-permute-start.1 = (bf16[128,4096]{0,1:T(8,128)(2,1)}, bf16[128,4096]{0,1:T(8,128)(2,1)S(1)}, u32[]{:S(2)}, u32[]{:S(2)}) collective-permute-start(bf16[128,4096]{0,1:T(8,128)(2,1)} %get-tuple-element.621), channel_id=1, source_target_pairs={{0,8},{8,16},{16,24},{24,32},{32,40},{40,48},{48,56},{56,64},{64,7... | collective-permute-start | bytes 3145736 | tf_op jit(solution)/shard_map/while/body/eval_jaxpr/ppermute | solution.py:15
  1131.0 19.6 %collective-permute-start.1 = (bf16[128,4096]{0,1:T(8,128)(2,1)}, bf16[128,4096]{0,1:T(8,128)(2,1)S(1)}, u32[]{:S(2)}, u32[]{:S(2)}) collective-permute-start(bf16[128,4096]{0,1:T(8,128)(2,1)} %get-tuple-element.621), channel_id=1, source_target_pairs={{0,8},{8,16},{16,24},{24,32},{32,40},{40,48},{48,56},{56,64},{64,7... | collective-permute-start | bytes 3145736 | tf_op jit(solution)/shard_map/while/body/eval_jaxpr/ppermute | solution.py:15
  1164.6 18.7 %collective-permute-start.1 = (bf16[128,4096]{0,1:T(8,128)(2,1)}, bf16[128,4096]{0,1:T(8,128)(2,1)S(1)}, u32[]{:S(2)}, u32[]{:S(2)}) collective-permute-start(bf16[128,4096]{0,1:T(8,128)(2,1)} %get-tuple-element.621), channel_id=1, source_target_pairs={{0,8},{8,16},{16,24},{24,32},{32,40},{40,48},{48,56},{56,64},{64,7... | collective-permute-start | bytes 3145736 | tf_op jit(solution)/shard_map/while/body/eval_jaxpr/ppermute | solution.py:15
  1197.3 17.8 %collective-permute-start.1 = (bf16[128,4096]{0,1:T(8,128)(2,1)}, bf16[128,4096]{0,1:T(8,128)(2,1)S(1)}, u32[]{:S(2)}, u32[]{:S(2)}) collective-permute-start(bf16[128,4096]{0,1:T(8,128)(2,1)} %get-tuple-element.621), channel_id=1, source_target_pairs={{0,8},{8,16},{16,24},{24,32},{32,40},{40,48},{48,56},{56,64},{64,7... | collective-permute-start | bytes 3145736 | tf_op jit(solution)/shard_map/while/body/eval_jaxpr/ppermute | solution.py:15
  1229.1 17.8 %collective-permute-start.1 = (bf16[128,4096]{0,1:T(8,128)(2,1)}, bf16[128,4096]{0,1:T(8,128)(2,1)S(1)}, u32[]{:S(2)}, u32[]{:S(2)}) collective-permute-start(bf16[128,4096]{0,1:T(8,128)(2,1)} %get-tuple-element.621), channel_id=1, source_target_pairs={{0,8},{8,16},{16,24},{24,32},{32,40},{40,48},{48,56},{56,64},{64,7... | collective-permute-start | bytes 3145736 | tf_op jit(solution)/shard_map/while/body/eval_jaxpr/ppermute | solution.py:15
  1261.0 17.8 %collective-permute-start.1 = (bf16[128,4096]{0,1:T(8,128)(2,1)}, bf16[128,4096]{0,1:T(8,128)(2,1)S(1)}, u32[]{:S(2)}, u32[]{:S(2)}) collective-permute-start(bf16[128,4096]{0,1:T(8,128)(2,1)} %get-tuple-element.621), channel_id=1, source_target_pairs={{0,8},{8,16},{16,24},{24,32},{32,40},{40,48},{48,56},{56,64},{64,7... | collective-permute-start | bytes 3145736 | tf_op jit(solution)/shard_map/while/body/eval_jaxpr/ppermute | solution.py:15
  1292.8 17.8 %collective-permute-start.1 = (bf16[128,4096]{0,1:T(8,128)(2,1)}, bf16[128,4096]{0,1:T(8,128)(2,1)S(1)}, u32[]{:S(2)}, u32[]{:S(2)}) collective-permute-start(bf16[128,4096]{0,1:T(8,128)(2,1)} %get-tuple-element.621), channel_id=1, source_target_pairs={{0,8},{8,16},{16,24},{24,32},{32,40},{40,48},{48,56},{56,64},{64,7... | collective-permute-start | bytes 3145736 | tf_op jit(solution)/shard_map/while/body/eval_jaxpr/ppermute | solution.py:15
  1324.7 17.8 %collective-permute-start.1 = (bf16[128,4096]{0,1:T(8,128)(2,1)}, bf16[128,4096]{0,1:T(8,128)(2,1)S(1)}, u32[]{:S(2)}, u32[]{:S(2)}) collective-permute-start(bf16[128,4096]{0,1:T(8,128)(2,1)} %get-tuple-element.621), channel_id=1, source_target_pairs={{0,8},{8,16},{16,24},{24,32},{32,40},{40,48},{48,56},{56,64},{64,7... | collective-permute-start | bytes 3145736 | tf_op jit(solution)/shard_map/while/body/eval_jaxpr/ppermute | solution.py:15
where the time goes:
time: 1370 us; the launch traced here: 1350 us
  waiting for transfers between devices  540 us (39%)
  other arithmetic  273 us (20%)
  local copies, waits for them, and re-layouts  158 us (12%)
  starting transfers between devices  151 us (11%)
  matrix products  142 us (10%)
  blocking collectives  77.2 us (6%)
    ppermute x34, waiting for transfers between devices, passed_along(): lax.ppermute(value, axis, [(source, source + steps) for source in range(l...  540 us
    ppermute x34, starting transfers between devices, passed_along(): lax.ppermute(value, axis, [(source, source + steps) for source in range(l...  151 us
    dot_general x40, matrix products, preact(): jnp.einsum('rnki,nkio->rno', picked, weight, preferred_element_type=jnp.f...  142 us
    gather x40, local copies, waits for them, and re-layouts, preact(): jnp.take(blocks, pattern.reshape(-1), axis=1)  121 us
    select_n x32, other arithmetic, turn(): result = jnp.where(index == step, value, result)  106 us
    select_n x76, other arithmetic, preact(): jnp.take(blocks, pattern.reshape(-1), axis=1)  105 us
    psum x1, blocking collectives, on_device(): total = lax.psum(jnp.sum(diff * diff), ('layer', 'batch'))  77.2 us
    select_n x32, other arithmetic, turn(): source = jnp.where(index == 0, inputs, incoming)  43 us
  transfers between devices with their start and end apart: 34, of which 33 were waited for; matrix products, arithmetic and copies ran while one was open for 2% of the time, Pallas kernels for 0%

commit v1 on v0

v1 whole, which is shorter than its diff:
```python
import functools

import jax
import jax.numpy as jnp
from jax import lax
from jax.experimental import pallas as pl
from jax.experimental.pallas import tpu as pltpu
from jax.sharding import PartitionSpec as P

MESH = pl.DeviceIdType.MESH
STEP = 0.25
ITERS = 2
ROWS = 8
PAIR = 2
BLOCK = 128


def kernel(chain, pat, inputs, warm, weights, bias, out, sums, w, start, own, c1, c2, e1, e2, tau,
           xs, xa, xb, gc, ref, comb, acc, w_sem, own_sem, start_send, start_recv, c1_send, c1_recv,
           c2_send, c2_recv, out_sem):
    me = lax.axis_index("layer")
    nxt, prv = lax.rem(me + 1, chain), lax.rem(me + chain - 1, chain)
    layers, blocks, picks = weights.shape[0], weights.shape[1], 4
    factor = layers * STEP
    chunks = inputs.shape[0]
    pairs = chunks // PAIR
    first, second, last = me == 0, me == 1, me == chain - 1
    rows = PAIR * ROWS

    def to_next(src, dst, send, recv):
        return pltpu.make_async_remote_copy(
            src_ref=src, dst_ref=dst, send_sem=send, recv_sem=recv,
            device_id={"layer": nxt}, device_id_type=MESH)

    def weight_copy(layer):
        return pltpu.make_async_copy(weights.at[layer], w.at[layer], w_sem.at[layer])

    def own_copy(j):
        return pltpu.make_async_copy(warm.at[j], own.at[j], own_sem.at[j])

    def input_copy(j):
        return pltpu.make_async_copy(inputs.at[j], start.at[j], start_recv.at[j])

    def warm_send(j):
        return to_next(warm.at[j], start.at[j], start_send.at[j], start_recv.at[j])

    def c1_copy(j):
        return to_next(e1.at[j], c1.at[j], c1_send.at[j], c1_recv.at[j])

    def c2_copy(j):
        return to_next(e2.at[j], c2.at[j], c2_send.at[j], c2_recv.at[j])

    def out_copy(j, buf):
        return pltpu.make_async_copy(buf.at[j], out.at[j], out_sem.at[j])

    def each(count, do):
        def body(j, carry):
            do(j)
            return carry
        lax.fori_loop(0, count, body, 0)

    weight_copy(0).start()

    @pl.when(first)
    def _():
        each(chunks, lambda j: input_copy(j).start())

    each(chunks, lambda j: own_copy(j).start())
    for layer in range(1, layers):
        weight_copy(layer).start()

    barrier = pltpu.get_barrier_semaphore()
    for neighbour in (nxt, prv):
        pl.semaphore_signal(barrier, inc=1, device_id={"layer": neighbour}, device_id_type=MESH)
    pl.semaphore_wait(barrier, 2)

    @pl.when(jnp.logical_not(last))
    def _():
        each(chunks, lambda j: warm_send(j).start())

    acc[...] = jnp.zeros_like(acc)

    def layer_of(layer, src, epilogue, unroll=True):
        def body(c, carry):
            at = (layer * blocks + c) * picks
            taken = [src[pat[at + k]] for k in range(picks)]
            pre = jnp.dot(jnp.concatenate(taken, axis=1), w[layer, c],
                          preferred_element_type=jnp.float32)
            epilogue(c, jnp.tanh(pre + bias[layer, c]))
            return carry
        lax.fori_loop(0, blocks, body, 0, unroll=unroll)

    def fold(x):
        return jnp.sum(x.reshape(rows // 8, 8, BLOCK), axis=0)

    def relax_first(p):
        for i in range(PAIR):
            j = p * PAIR + i

            @pl.when(first)
            def _():
                input_copy(j).wait()

            @pl.when(jnp.logical_not(first))
            def _():
                warm_send(j).wait_recv()

            own_copy(j).wait()
        x = [start[p * PAIR + i].astype(jnp.float32) for i in range(PAIR)]
        xa[...] = jnp.concatenate(x, axis=1).astype(jnp.bfloat16)
        for i in range(PAIR):
            ref[:, i * ROWS:(i + 1) * ROWS] = own[p * PAIR + i].astype(jnp.float32)

        def epilogue(c, t):
            x = xa[c].astype(jnp.float32)
            gc[c] = x + factor * t
            xb[c] = (x + STEP * t).astype(jnp.bfloat16)
        layer_of(0, xa, epilogue, 16)

    def sweep_first(p):
        def chunk(i, carry):
            j = p * PAIR + i
            c1_copy(j).wait_recv()
            xs[...] = c1[j]
            at_rows = pl.ds(pl.multiple_of(i * ROWS, ROWS), ROWS)

            def epilogue(c, t):
                x = xs[c].astype(jnp.float32)
                coarse = x + factor * t
                end = (coarse + tau[j, c]).astype(jnp.bfloat16)
                e1[j, c] = end
                gc[c, at_rows] = coarse
                ref[c, at_rows] = end.astype(jnp.float32)
                comb[c, at_rows] = x + STEP * t
            layer_of(0, xs, epilogue)

            @pl.when(jnp.logical_not(last))
            def _():
                c1_copy(j).start()
            return carry
        lax.fori_loop(0, PAIR, chunk, 0)
        xb[...] = comb[...].astype(jnp.bfloat16)

    def fine(p, phase):
        src, dst = xb, xa
        for layer in range(1, layers - 1):
            def middle(c, t, src=src, dst=dst):
                dst[c] = (src[c].astype(jnp.float32) + STEP * t).astype(jnp.bfloat16)
            layer_of(layer, src, middle)
            src, dst = dst, src

        def epilogue(c, t):
            g = (src[c].astype(jnp.float32) + STEP * t).astype(jnp.bfloat16).astype(jnp.float32)
            coarse = gc[c]
            correction = g - coarse
            joined = (coarse + correction).astype(jnp.bfloat16).astype(jnp.float32)
            for i in range(PAIR):
                tau[p * PAIR + i, c] = correction[i * ROWS:(i + 1) * ROWS]
            comb[c] = joined
            off = g - ref[c]
            acc[phase] += fold(off * off)
            off = g - joined
            acc[2] += fold(off * off)
        layer_of(layers - 1, src, epilogue)

    def sweep_second(p):
        def chunk(i, carry):
            j = p * PAIR + i
            c2_copy(j).wait_recv()
            xs[...] = c2[j]

            def epilogue(c, t):
                x = xs[c].astype(jnp.float32)
                e2[j, c] = (x + factor * t + tau[j, c]).astype(jnp.bfloat16)
            layer_of(0, xs, epilogue)

            @pl.when(jnp.logical_not(last))
            def _():
                c2_copy(j).start()
            out_copy(j, e2).start()
            return carry
        lax.fori_loop(0, PAIR, chunk, 0)

    for layer in range(layers):
        weight_copy(layer).wait()

    lead = jnp.minimum(pairs, lax.max(me - 1, 0) * 3 // 2)
    lead = jnp.where(first, 0, lead)

    def step(s, carry):
        p = s - lead

        def phase_of(phase, carry):
            run = jnp.where(phase == 0, s < pairs,
                            jnp.logical_and(p >= 0, jnp.logical_not(first)))
            q = jnp.where(phase == 0, s, p)

            @pl.when(run)
            def _():
                @pl.when(phase == 0)
                def _():
                    relax_first(q)

                @pl.when(phase == 1)
                def _():
                    sweep_first(q)

                fine(q, phase)

            return carry
        lax.fori_loop(0, ITERS, phase_of, 0)

        @pl.when(first)
        def _():
            for i in range(PAIR):
                j = s * PAIR + i
                e1[j] = comb[:, i * ROWS:(i + 1) * ROWS].astype(jnp.bfloat16)
                c1_copy(j).start()
                out_copy(j, e1).start()

        @pl.when(second)
        def _():
            for i in range(PAIR):
                j = p * PAIR + i
                e2[j] = comb[:, i * ROWS:(i + 1) * ROWS].astype(jnp.bfloat16)
                c2_copy(j).start()
                out_copy(j, e2).start()

        @pl.when(jnp.logical_and(me >= 2, p >= 0))
        def _():
            sweep_second(p)

        return carry

    lax.fori_loop(0, pairs + lead, step, 0)

    sums[0] = acc[0]
    sums[1] = jnp.where(first, acc[2], acc[1])

    @pl.when(jnp.logical_not(last))
    def _():
        each(chunks, lambda j: warm_send(j).wait_send())
        each(chunks, lambda j: c1_copy(j).wait_send())

    @pl.when(jnp.logical_and(jnp.logical_not(last), jnp.logical_not(first)))
    def _():
        each(chunks, lambda j: c2_copy(j).wait_send())

    each(chunks, lambda j: out_copy(j, e2).wait())


def on_device(inputs, warm_states, weights, pattern, bias):
    chain = lax.axis_size("layer")
    rows, width = inputs.shape
    layers, blocks, picks, size, _ = weights.shape
    chunks = rows // ROWS
    count = float(chain * lax.axis_size("batch") * rows * width)

    def pieces(x):
        return x.reshape(chunks, ROWS, blocks, size).transpose(0, 2, 1, 3)

    any_ = pl.BlockSpec(memory_space=pl.ANY)
    vmem = pl.BlockSpec(memory_space=pltpu.VMEM)
    piece = (chunks, blocks, ROWS, size)
    dma = pltpu.SemaphoreType.DMA
    ends, sums = pl.pallas_call(
        functools.partial(kernel, chain),
        out_shape=(
            jax.ShapeDtypeStruct(piece, jnp.bfloat16),
            jax.ShapeDtypeStruct((ITERS, 8, BLOCK), jnp.float32),
        ),
        in_specs=[pl.BlockSpec(memory_space=pltpu.SMEM), any_, any_, any_, vmem],
        out_specs=(any_, vmem),
        scratch_shapes=[
            pltpu.VMEM((layers, blocks, picks * size, size), jnp.bfloat16),
            *[pltpu.VMEM(piece, jnp.bfloat16)] * 6,
            pltpu.VMEM(piece, jnp.float32),
            pltpu.VMEM((blocks, ROWS, size), jnp.bfloat16),
            *[pltpu.VMEM((blocks, PAIR * ROWS, size), jnp.bfloat16)] * 2,
            *[pltpu.VMEM((blocks, PAIR * ROWS, size), jnp.float32)] * 3,
            pltpu.VMEM((3, 8, BLOCK), jnp.float32),
            dma((layers,)),
            *[dma((chunks,))] * 8,
        ],
        compiler_params=pltpu.CompilerParams(
            collective_id=0, has_side_effects=True, vmem_limit_bytes=60 << 20),
    )(
        pattern.reshape(-1),
        pieces(inputs),
        pieces(warm_states),
        weights.reshape(layers, blocks, picks * size, size),
        bias.reshape(layers, blocks, 1, size),
    )
    total = lax.psum(jnp.sum(sums, axis=(1, 2)), ("layer", "batch"))
    ends = ends.transpose(0, 2, 1, 3).reshape(1, rows, width)
    return ends, jnp.sqrt(total / count)


def solution(mesh):
    in_specs = (
        P("batch", None),
        P("layer", "batch", None),
        P("layer", None, None, None, None),
        P("layer", None, None),
        P("layer", None),
    )
    return jax.shard_map(
        on_device, mesh=mesh, in_specs=in_specs,
        out_specs=(P("layer", "batch", None), P()), check_vma=False)
```

time: 1370 us -> 228 us (0.17); the launches traced: 1350 us -> 227 us
  waiting for transfers between devices: 540 us -> 0 us
  other arithmetic: 273 us -> 1.32 us
  local copies, waits for them, and re-layouts: 158 us -> 5.35 us
  starting transfers between devices: 151 us -> 0 us
  matrix products: 142 us -> 0 us
  blocking collectives: 77.2 us -> 165 us
  Pallas kernels: 0 us -> 54.5 us
    ppermute x34 -> x0, waiting for transfers between devices: 540 us -> none  [passed_along(): lax.ppermute(value, axis, [(source, source + steps) for source in range(l...]
    select_n x142 -> x0, other arithmetic: 257 us -> none  [the longest x32 106 us: turn(): result = jnp.where(index == step, value, result)]
    ppermute x34 -> x0, starting transfers between devices: 151 us -> none  [passed_along(): lax.ppermute(value, axis, [(source, source + steps) for source in range(l...]
    dot_general x40 -> x0, matrix products: 142 us -> none  [preact(): jnp.einsum('rnki,nkio->rno', picked, weight, preferred_element_type=jnp.f...]
    gather x40 -> x0, local copies, waits for them, and re-layouts: 121 us -> none  [preact(): jnp.take(blocks, pattern.reshape(-1), axis=1)]
    psum x1, blocking collectives: 77.2 us -> 165 us  [on_device(): total = lax.psum(jnp.sum(sums, axis=(1, 2)), ('layer', 'batch'))]
    pallas_call x0 -> x1, Pallas kernels: none -> 54.5 us  [on_device(): pl.pallas_call(functools.partial(kernel, chain), out_shape=(jax.ShapeDtyp...]
    while x4 -> x0, local copies, waits for them, and re-layouts: 26.6 us -> none  [on_device(): _, ends = lax.fori_loop(0, chain_len, turn, (jnp.zeros_like(ends), ends))]
  transfers between devices with their start and end apart: 34 -> 0, of which waited for: 33 -> 0; matrix products, arithmetic and copies ran while one was open for 2% -> 0% of each run, Pallas kernels for 0% -> 0%
where the time goes in v1:
time: 228 us; the launch traced here: 227 us
  blocking collectives  165 us (72%)
  Pallas kernels  54.5 us (24%)
  local copies, waits for them, and re-layouts  5.35 us (2%)
    psum x1, blocking collectives, on_device(): total = lax.psum(jnp.sum(sums, axis=(1, 2)), ('layer', 'batch'))  165 us
    pallas_call x1, Pallas kernels, on_device(): pl.pallas_call(functools.partial(kernel, chain), out_shape=(jax.ShapeDtyp...  54.5 us

profile of v1, /device:TPU:0, one launch (start us, length us, event | category | flops | bytes accessed | tf_op | source)
XLA Modules:
  0.0 227.2 jit_solution(3519272967308447869)
XLA Ops:
  0.6 0.8 copy.7
  1.4 0.7 reshape.22.pat
  2.1 1.6 reshape.26.bias
  3.7 54.5 %shard_map.68 = (bf16[16,32,8,128]{3,2,1,0:T(8,128)(2,1)}, f32[2,8,128]{2,1,0:T(8,128)}) custom-call(s32[512]{0:T(512)} %reshape.22.pat, bf16[16,32,8,128]{3,2,1,0:T(8,128)(2,1)} %bitcast.11, bf16[16,32,8,128]{3,2,1,0:T(8,128)(2,1)} %bitcast.12, bf16[4,32,512,128]{3,2,1,0:T(8,128)(2,1)} %bitcast.10, f32[4,32,1,128]{3,2,1,0:T(1,128)} %reshape.26.bias), custom_call_target="tpu_custom_call" | custom-call | tf_op jit(solution)/shard_map/pallas_call | solution.py:266
  58.2 0.8 reduce_sum.9
  59.0 165.4 %psum.7 = f32[2]{0:T(128)S(1)} all-reduce(f32[2]{0:T(128)S(1)} %reduce_sum.9), channel_id=1, replica_groups=mesh['layer'=16,'batch'=8] {'layer','batch'}, use_global_device_ids=true, to_apply=%region_1.0 | all-reduce | flops 2 | bytes 16 | tf_op jit(solution)/shard_map/psum | solution.py:294
  224.4 0.5 multiply_sqrt_fusion
  224.9 2.3 %copy.9 = bf16[1,128,4096]{2,1,0:T(8,128)(2,1)} copy(bf16[1,128,4096]{2,1,0:T(8,128)(2,1)} %bitcast.13) | data formatting | bytes 2097152

commit v2 on v1

--- a/solution.py
+++ b/solution.py
@@ -15,10 +15,12 @@
 BLOCK = 128
 
 
-def kernel(chain, pat, inputs, warm, weights, bias, out, sums, w, start, own, c1, c2, e1, e2, tau,
-           xs, xa, xb, gc, ref, comb, acc, w_sem, own_sem, start_send, start_recv, c1_send, c1_recv,
-           c2_send, c2_recv, out_sem):
+def kernel(chain, peers, pat, inputs, warm, weights, bias, out, norms, w, start, own, c1, c2, e1, e2, tau,
+           xs, xa, xb, gc, ref, comb, acc, part, before, around, total, w_sem, own_sem, start_send, start_recv, c1_send, c1_recv,
+           c2_send, c2_recv, out_sem,
+           part_send, part_recv, peer_send, peer_recv, total_send, total_recv):
     me = lax.axis_index("layer")
+    mine = lax.axis_index("batch")
     nxt, prv = lax.rem(me + 1, chain), lax.rem(me + chain - 1, chain)
     layers, blocks, picks = weights.shape[0], weights.shape[1], 4
     factor = layers * STEP
@@ -50,6 +52,20 @@
     def c2_copy(j):
         return to_next(e2.at[j], c2.at[j], c2_send.at[j], c2_recv.at[j])
 
+    def part_copy():
+        return to_next(part, before, part_send, part_recv)
+
+    def peer_copy(hop):
+        return pltpu.make_async_remote_copy(
+            src_ref=part, dst_ref=around.at[hop - 1], send_sem=peer_send.at[hop - 1],
+            recv_sem=peer_recv.at[hop - 1],
+            device_id={"batch": lax.rem(mine + hop, peers)}, device_id_type=MESH)
+
+    def total_copy(layer):
+        return pltpu.make_async_remote_copy(
+            src_ref=part, dst_ref=total, send_sem=total_send.at[layer], recv_sem=total_recv,
+            device_id={"layer": layer}, device_id_type=MESH)
+
     def out_copy(j, buf):
         return pltpu.make_async_copy(buf.at[j], out.at[j], out_sem.at[j])
 
@@ -70,23 +86,34 @@
         weight_copy(layer).start()
 
     barrier = pltpu.get_barrier_semaphore()
-    for neighbour in (nxt, prv):
-        pl.semaphore_signal(barrier, inc=1, device_id={"layer": neighbour}, device_id_type=MESH)
-    pl.semaphore_wait(barrier, 2)
+
+    def greet(**device):
+        pl.semaphore_signal(barrier, inc=1, device_id=device, device_id_type=MESH)
+
+    @pl.when(jnp.logical_not(first))
+    def _():
+        greet(layer=prv)
 
     @pl.when(jnp.logical_not(last))
     def _():
+        greet(layer=chain - 1)
+        pl.semaphore_wait(barrier, 1)
         each(chunks, lambda j: warm_send(j).start())
+
+    @pl.when(last)
+    def _():
+        for hop in range(1, peers):
+            greet(batch=lax.rem(mine + hop, peers))
+        pl.semaphore_wait(barrier, chain - 1 + peers - 1)
 
     acc[...] = jnp.zeros_like(acc)
 
     def layer_of(layer, src, epilogue, unroll=True):
         def body(c, carry):
-            at = (layer * blocks + c) * picks
-            taken = [src[pat[at + k]] for k in range(picks)]
+            taken = [src[pat[layer, k, c]] for k in range(picks)]
             pre = jnp.dot(jnp.concatenate(taken, axis=1), w[layer, c],
                           preferred_element_type=jnp.float32)
-            epilogue(c, jnp.tanh(pre + bias[layer, c]))
+            epilogue(c, jnp.tanh(pre + bias[layer:layer + 1, pl.ds(c * BLOCK, BLOCK)]))
             return carry
         lax.fori_loop(0, blocks, body, 0, unroll=unroll)
 
@@ -210,6 +237,25 @@
             return carry
         lax.fori_loop(0, ITERS, phase_of, 0)
 
+        @pl.when(s == pairs + lead - 1)
+        def _():
+            part[0] = acc[0]
+            part[1] = jnp.where(first, acc[2], acc[1])
+
+            @pl.when(jnp.logical_not(first))
+            def _():
+                part_copy().wait_recv()
+                part[...] += before[...]
+
+            @pl.when(jnp.logical_not(last))
+            def _():
+                part_copy().start()
+
+            @pl.when(last)
+            def _():
+                for hop in range(1, peers):
+                    peer_copy(hop).start()
+
         @pl.when(first)
         def _():
             for i in range(PAIR):
@@ -234,11 +280,21 @@
 
     lax.fori_loop(0, pairs + lead, step, 0)
 
-    sums[0] = acc[0]
-    sums[1] = jnp.where(first, acc[2], acc[1])
+    @pl.when(last)
+    def _():
+        for hop in range(1, peers):
+            peer_copy(hop).wait()
+        part[...] += jnp.sum(around[...], axis=0)
+        for layer in range(chain - 1):
+            total_copy(layer).start()
+        total[...] = part[...]
+        for layer in range(chain - 1):
+            total_copy(layer).wait_send()
 
     @pl.when(jnp.logical_not(last))
     def _():
+        part_copy().wait_send()
+        total_copy(0).wait_recv()
         each(chunks, lambda j: warm_send(j).wait_send())
         each(chunks, lambda j: c1_copy(j).wait_send())
 
@@ -247,6 +303,8 @@
         each(chunks, lambda j: c2_copy(j).wait_send())
 
     each(chunks, lambda j: out_copy(j, e2).wait())
+    for i in range(ITERS):
+        norms[i] = jnp.sum(total[i])
 
 
 def on_device(inputs, warm_states, weights, pattern, bias):
@@ -263,14 +321,15 @@
     vmem = pl.BlockSpec(memory_space=pltpu.VMEM)
     piece = (chunks, blocks, ROWS, size)
     dma = pltpu.SemaphoreType.DMA
-    ends, sums = pl.pallas_call(
-        functools.partial(kernel, chain),
+    peers = lax.axis_size("batch")
+    ends, norms = pl.pallas_call(
+        functools.partial(kernel, chain, peers),
         out_shape=(
             jax.ShapeDtypeStruct(piece, jnp.bfloat16),
-            jax.ShapeDtypeStruct((ITERS, 8, BLOCK), jnp.float32),
+            jax.ShapeDtypeStruct((ITERS,), jnp.float32),
         ),
         in_specs=[pl.BlockSpec(memory_space=pltpu.SMEM), any_, any_, any_, vmem],
-        out_specs=(any_, vmem),
+        out_specs=(any_, pl.BlockSpec(memory_space=pltpu.SMEM)),
         scratch_shapes=[
             pltpu.VMEM((layers, blocks, picks * size, size), jnp.bfloat16),
             *[pltpu.VMEM(piece, jnp.bfloat16)] * 6,
@@ -279,21 +338,24 @@
             *[pltpu.VMEM((blocks, PAIR * ROWS, size), jnp.bfloat16)] * 2,
             *[pltpu.VMEM((blocks, PAIR * ROWS, size), jnp.float32)] * 3,
             pltpu.VMEM((3, 8, BLOCK), jnp.float32),
+            *[pltpu.VMEM((ITERS, 8, BLOCK), jnp.float32)] * 2,
+            pltpu.VMEM((peers - 1, ITERS, 8, BLOCK), jnp.float32),
+            pltpu.VMEM((ITERS, 8, BLOCK), jnp.float32),
             dma((layers,)),
             *[dma((chunks,))] * 8,
+            dma, dma, dma((peers - 1,)), dma((peers - 1,)), dma((chain - 1,)), dma,
         ],
         compiler_params=pltpu.CompilerParams(
             collective_id=0, has_side_effects=True, vmem_limit_bytes=60 << 20),
     )(
-        pattern.reshape(-1),
+        pattern.transpose(0, 2, 1),
         pieces(inputs),
         pieces(warm_states),
         weights.reshape(layers, blocks, picks * size, size),
-        bias.reshape(layers, blocks, 1, size),
+        bias,
     )
-    total = lax.psum(jnp.sum(sums, axis=(1, 2)), ("layer", "batch"))
     ends = ends.transpose(0, 2, 1, 3).reshape(1, rows, width)
-    return ends, jnp.sqrt(total / count)
+    return ends, jnp.sqrt(norms / count)
 
 
 def solution(mesh):

time: 228 us -> 165 us (0.72)
  blocking collectives: 165 us -> 0 us
  Pallas kernels: 54.5 us -> 161 us
  local copies, waits for them, and re-layouts: 5.35 us -> 2.29 us
    psum x1 -> x0, blocking collectives: 165 us -> none  [on_device(): total = lax.psum(jnp.sum(sums, axis=(1, 2)), ('layer', 'batch'))]
    pallas_call x1, Pallas kernels: 54.5 us -> 161 us  [on_device(): pl.pallas_call(functools.partial(kernel, chain, peers), out_shape=(jax.Sh...]
where the time goes in v2:
time: 165 us
  Pallas kernels  161 us (98%)
  local copies, waits for them, and re-layouts  2.29 us (1%)
    pallas_call x1, Pallas kernels, on_device(): pl.pallas_call(functools.partial(kernel, chain, peers), out_shape=(jax.Sh...  161 us

profile of v2, /device:TPU:0, one launch (start us, length us, event | category | flops | bytes accessed | tf_op | source)
XLA Modules:
  0.0 164.6 jit_solution(5158848832910493167)
XLA Ops:
  0.6 160.6 %shard_map.68 = (bf16[16,32,8,128]{3,2,1,0:T(8,128)(2,1)}, f32[2]{0:T(128)}) custom-call(s32[4,4,32]{2,1,0:T(4,128)} %bitcast.15, bf16[16,32,8,128]{3,2,1,0:T(8,128)(2,1)} %bitcast.12, bf16[16,32,8,128]{3,2,1,0:T(8,128)(2,1)} %bitcast.13, bf16[4,32,512,128]{3,2,1,0:T(8,128)(2,1)} %bitcast.11, f32[4,4096]{1,0:T(4,128)} %bias.1), custom_call_target="tpu_custom_call" | custom-call | tf_op jit(solution)/shard_map/pallas_call | solution.py:325
  161.2 1.1 multiply_sqrt_fusion
  162.3 2.3 %copy.8 = bf16[1,128,4096]{2,1,0:T(8,128)(2,1)} copy(bf16[1,128,4096]{2,1,0:T(8,128)(2,1)} %bitcast.14) | data formatting | bytes 2097152

commit v3 on v2

--- a/solution.py
+++ b/solution.py
@@ -12,11 +12,15 @@
 ITERS = 2
 ROWS = 8
 PAIR = 2
+QUAD = 4
+DIRECT = 2
+SIDE = 4
 BLOCK = 128
 
 
-def kernel(chain, peers, pat, inputs, warm, weights, bias, out, norms, w, start, own, c1, c2, e1, e2, tau,
-           xs, xa, xb, gc, ref, comb, acc, part, before, around, total, w_sem, own_sem, start_send, start_recv, c1_send, c1_recv,
+def kernel(chain, peers, pat, inputs, warm, weights, bias, out, norms, w, start, own, c1, c2, e1, e2, hold, tau,
+           xs, xa, xb, gc, ref, comb, ya, yb, gy, acc, part, before, around, total, w_sem, own_sem, start_send, start_recv,
+           hold_send, hold_recv, c1_send, c1_recv,
            c2_send, c2_recv, out_sem,
            part_send, part_recv, peer_send, peer_recv, total_send, total_recv):
     me = lax.axis_index("layer")
@@ -27,7 +31,11 @@
     chunks = inputs.shape[0]
     pairs = chunks // PAIR
     first, second, last = me == 0, me == 1, me == chain - 1
-    rows = PAIR * ROWS
+    sender = me < SIDE
+    aside = jnp.where(me < SIDE - 1, chain - SIDE + 1 + me, 0)
+    late = me > chain - SIDE
+    relay = jnp.logical_or(late, first)
+    target = jnp.where(first, SIDE, jnp.where(late, me - (chain - SIDE), me))
 
     def to_next(src, dst, send, recv):
         return pltpu.make_async_remote_copy(
@@ -37,14 +45,27 @@
     def weight_copy(layer):
         return pltpu.make_async_copy(weights.at[layer], w.at[layer], w_sem.at[layer])
 
-    def own_copy(j):
-        return pltpu.make_async_copy(warm.at[j], own.at[j], own_sem.at[j])
-
-    def input_copy(j):
-        return pltpu.make_async_copy(inputs.at[j], start.at[j], start_recv.at[j])
-
-    def warm_send(j):
-        return to_next(warm.at[j], start.at[j], start_send.at[j], start_recv.at[j])
+    def pair(ref, p):
+        return ref.at[pl.ds(p * PAIR, PAIR)]
+
+    def own_copy(p):
+        return pltpu.make_async_copy(pair(warm, p), pair(own, p), own_sem.at[p])
+
+    def input_copy(p):
+        return pltpu.make_async_copy(pair(inputs, p), pair(start, p), start_recv.at[p])
+
+    def warm_send(p):
+        return to_next(pair(warm, p), pair(start, p), start_send.at[p], start_recv.at[p])
+
+    def warm_aside(p):
+        return pltpu.make_async_remote_copy(
+            src_ref=pair(warm, p), dst_ref=pair(hold, p), send_sem=start_send.at[p],
+            recv_sem=hold_recv.at[p], device_id={"layer": aside}, device_id_type=MESH)
+
+    def warm_back(p):
+        return pltpu.make_async_remote_copy(
+            src_ref=pair(hold, p), dst_ref=pair(start, p), send_sem=hold_send.at[p],
+            recv_sem=start_recv.at[p], device_id={"layer": target}, device_id_type=MESH)
 
     def c1_copy(j):
         return to_next(e1.at[j], c1.at[j], c1_send.at[j], c1_recv.at[j])
@@ -79,9 +100,9 @@
 
     @pl.when(first)
     def _():
-        each(chunks, lambda j: input_copy(j).start())
-
-    each(chunks, lambda j: own_copy(j).start())
+        each(pairs, lambda p: input_copy(p).start())
+
+    each(pairs, lambda p: own_copy(p).start())
     for layer in range(1, layers):
         weight_copy(layer).start()
 
@@ -97,14 +118,46 @@
     @pl.when(jnp.logical_not(last))
     def _():
         greet(layer=chain - 1)
-        pl.semaphore_wait(barrier, 1)
-        each(chunks, lambda j: warm_send(j).start())
 
     @pl.when(last)
     def _():
         for hop in range(1, peers):
             greet(batch=lax.rem(mine + hop, peers))
-        pl.semaphore_wait(barrier, chain - 1 + peers - 1)
+
+    @pl.when(relay)
+    def _():
+        greet(layer=jnp.where(first, SIDE - 1, target - 1))
+
+    @pl.when(jnp.logical_and(me >= 1, me <= SIDE))
+    def _():
+        greet(layer=jnp.where(me == SIDE, 0, me + chain - SIDE))
+
+    def one(flag):
+        return jnp.where(flag, 1, 0)
+
+    pl.semaphore_wait(barrier, one(sender) + one(relay)
+                      + jnp.where(last, chain - 1 + peers - 1, 1))
+
+    @pl.when(jnp.logical_and(me < chain - SIDE, jnp.logical_not(sender)))
+    def _():
+        each(pairs, lambda p: warm_send(p).start())
+
+    @pl.when(sender)
+    def _():
+        each(DIRECT, lambda p: warm_send(p).start())
+        each(pairs - DIRECT, lambda p: warm_aside(p + DIRECT).start())
+
+    def pass_on(p):
+        warm_aside(p).wait_recv()
+        warm_back(p).start()
+
+    @pl.when(late)
+    def _():
+        each(pairs - DIRECT, lambda p: pass_on(p + DIRECT))
+
+    @pl.when(jnp.logical_and(late, jnp.logical_not(last)))
+    def _():
+        each(pairs, lambda p: warm_send(p).start())
 
     acc[...] = jnp.zeros_like(acc)
 
@@ -118,31 +171,53 @@
         lax.fori_loop(0, blocks, body, 0, unroll=unroll)
 
     def fold(x):
-        return jnp.sum(x.reshape(rows // 8, 8, BLOCK), axis=0)
-
-    def relax_first(p):
-        for i in range(PAIR):
-            j = p * PAIR + i
+        return jnp.sum(x.reshape(x.shape[0] // 8, 8, BLOCK), axis=0)
+
+    def fine(src, dst, final):
+        for layer in range(1, layers - 1):
+            def middle(c, t, src=src, dst=dst):
+                dst[c] = (src[c].astype(jnp.float32) + STEP * t).astype(jnp.bfloat16)
+            layer_of(layer, src, middle)
+            src, dst = dst, src
+        layer_of(layers - 1, src, lambda c, t: final(c, src, t))
+
+    def relax_first(q):
+        for i in range(QUAD // PAIR):
+            p = q * (QUAD // PAIR) + i
 
             @pl.when(first)
             def _():
-                input_copy(j).wait()
+                input_copy(p).wait()
 
             @pl.when(jnp.logical_not(first))
             def _():
-                warm_send(j).wait_recv()
-
-            own_copy(j).wait()
-        x = [start[p * PAIR + i].astype(jnp.float32) for i in range(PAIR)]
-        xa[...] = jnp.concatenate(x, axis=1).astype(jnp.bfloat16)
-        for i in range(PAIR):
-            ref[:, i * ROWS:(i + 1) * ROWS] = own[p * PAIR + i].astype(jnp.float32)
-
-        def epilogue(c, t):
-            x = xa[c].astype(jnp.float32)
-            gc[c] = x + factor * t
-            xb[c] = (x + STEP * t).astype(jnp.bfloat16)
-        layer_of(0, xa, epilogue, 16)
+                warm_send(p).wait_recv()
+
+            own_copy(p).wait()
+        x = [start[q * QUAD + i].astype(jnp.float32) for i in range(QUAD)]
+        ya[...] = jnp.concatenate(x, axis=1).astype(jnp.bfloat16)
+
+        def entry(c, t):
+            x = ya[c].astype(jnp.float32)
+            gy[c] = x + factor * t
+            yb[c] = (x + STEP * t).astype(jnp.bfloat16)
+        layer_of(0, ya, entry, 16)
+
+        def final(c, src, t):
+            g = (src[c].astype(jnp.float32) + STEP * t).astype(jnp.bfloat16).astype(jnp.float32)
+            coarse = gy[c]
+            correction = g - coarse
+            joined = (coarse + correction).astype(jnp.bfloat16)
+            for i in range(QUAD):
+                j = q * QUAD + i
+                at_rows = slice(i * ROWS, (i + 1) * ROWS)
+                tau[j, c] = correction[at_rows]
+                e1[j, c] = joined[at_rows]
+                off = g[at_rows] - own[j, c].astype(jnp.float32)
+                acc[0] += off * off
+            off = g - joined.astype(jnp.float32)
+            acc[2] += fold(off * off)
+        fine(yb, ya, final)
 
     def sweep_first(p):
         def chunk(i, carry):
@@ -168,27 +243,19 @@
         lax.fori_loop(0, PAIR, chunk, 0)
         xb[...] = comb[...].astype(jnp.bfloat16)
 
-    def fine(p, phase):
-        src, dst = xb, xa
-        for layer in range(1, layers - 1):
-            def middle(c, t, src=src, dst=dst):
-                dst[c] = (src[c].astype(jnp.float32) + STEP * t).astype(jnp.bfloat16)
-            layer_of(layer, src, middle)
-            src, dst = dst, src
-
-        def epilogue(c, t):
+        def final(c, src, t):
             g = (src[c].astype(jnp.float32) + STEP * t).astype(jnp.bfloat16).astype(jnp.float32)
             coarse = gc[c]
             correction = g - coarse
-            joined = (coarse + correction).astype(jnp.bfloat16).astype(jnp.float32)
+            joined = (coarse + correction).astype(jnp.bfloat16)
             for i in range(PAIR):
-                tau[p * PAIR + i, c] = correction[i * ROWS:(i + 1) * ROWS]
-            comb[c] = joined
+                j = p * PAIR + i
+                at_rows = slice(i * ROWS, (i + 1) * ROWS)
+                tau[j, c] = correction[at_rows]
+                e2[j, c] = joined[at_rows]
             off = g - ref[c]
-            acc[phase] += fold(off * off)
-            off = g - joined
-            acc[2] += fold(off * off)
-        layer_of(layers - 1, src, epilogue)
+            acc[1] += fold(off * off)
+        fine(xb, xa, final)
 
     def sweep_second(p):
         def chunk(i, carry):
@@ -211,74 +278,78 @@
     for layer in range(layers):
         weight_copy(layer).wait()
 
-    lead = jnp.minimum(pairs, lax.max(me - 1, 0) * 3 // 2)
-    lead = jnp.where(first, 0, lead)
+    quads = chunks // QUAD
+    lead = jnp.where(first, quads, jnp.clip(2 * (me - SIDE) + 1, 0, quads))
+
+    def sweeps(p, carry):
+        sweep_first(p)
+
+        @pl.when(p == pairs - 1)
+        def _():
+            gather_part()
+
+        @pl.when(second)
+        def _():
+            for i in range(PAIR):
+                c2_copy(p * PAIR + i).start()
+                out_copy(p * PAIR + i, e2).start()
+
+        @pl.when(jnp.logical_not(second))
+        def _():
+            sweep_second(p)
+        return carry
+
+    def gather_part():
+        part[0] = acc[0]
+        part[1] = jnp.where(first, acc[2], acc[1])
+
+        @pl.when(jnp.logical_not(first))
+        def _():
+            part_copy().wait_recv()
+            part[...] += before[...]
+
+        @pl.when(jnp.logical_not(last))
+        def _():
+            part_copy().start()
+
+        @pl.when(last)
+        def _():
+            for hop in range(1, peers):
+                peer_copy(hop).start()
 
     def step(s, carry):
-        p = s - lead
-
-        def phase_of(phase, carry):
-            run = jnp.where(phase == 0, s < pairs,
-                            jnp.logical_and(p >= 0, jnp.logical_not(first)))
-            q = jnp.where(phase == 0, s, p)
-
-            @pl.when(run)
+        @pl.when(s < quads)
+        def _():
+            relax_first(s)
+
+            @pl.when(first)
             def _():
-                @pl.when(phase == 0)
-                def _():
-                    relax_first(q)
-
-                @pl.when(phase == 1)
-                def _():
-                    sweep_first(q)
-
-                fine(q, phase)
-
-            return carry
-        lax.fori_loop(0, ITERS, phase_of, 0)
-
-        @pl.when(s == pairs + lead - 1)
-        def _():
-            part[0] = acc[0]
-            part[1] = jnp.where(first, acc[2], acc[1])
-
-            @pl.when(jnp.logical_not(first))
-            def _():
-                part_copy().wait_recv()
-                part[...] += before[...]
-
-            @pl.when(jnp.logical_not(last))
-            def _():
-                part_copy().start()
-
-            @pl.when(last)
-            def _():
-                for hop in range(1, peers):
-                    peer_copy(hop).start()
-
-        @pl.when(first)
-        def _():
-            for i in range(PAIR):
-                j = s * PAIR + i
-                e1[j] = comb[:, i * ROWS:(i + 1) * ROWS].astype(jnp.bfloat16)
-                c1_copy(j).start()
-                out_copy(j, e1).start()
-
-        @pl.when(second)
-        def _():
-            for i in range(PAIR):
-                j = p * PAIR + i
-                e2[j] = comb[:, i * ROWS:(i + 1) * ROWS].astype(jnp.bfloat16)
-                c2_copy(j).start()
-                out_copy(j, e2).start()
-
-        @pl.when(jnp.logical_and(me >= 2, p >= 0))
-        def _():
-            sweep_second(p)
+                for i in range(QUAD):
+                    c1_copy(s * QUAD + i).start()
+                    out_copy(s * QUAD + i, e1).start()
+                for i in range(QUAD // PAIR):
+                    p = s * (QUAD // PAIR) + i
+
+                    @pl.when(p >= DIRECT)
+                    def _():
+                        pass_on(p)
+
+        @pl.when(jnp.logical_and(s == quads - 1, me == chain - SIDE))
+        def _():
+            each(pairs, lambda p: warm_send(p).start())
+
+        @pl.when(jnp.logical_and(s >= lead, jnp.logical_not(first)))
+        def _():
+            q = s - lead
+            lax.fori_loop(q * (QUAD // PAIR), (q + 1) * (QUAD // PAIR), sweeps, 0)
 
         return carry
 
-    lax.fori_loop(0, pairs + lead, step, 0)
+    lax.fori_loop(0, jnp.where(first, quads, quads + lead), step, 0)
+
+    @pl.when(first)
+    def _():
+        gather_part()
 
     @pl.when(last)
     def _():
@@ -295,12 +366,16 @@
     def _():
         part_copy().wait_send()
         total_copy(0).wait_recv()
-        each(chunks, lambda j: warm_send(j).wait_send())
+        each(pairs, lambda p: warm_send(p).wait_send())
         each(chunks, lambda j: c1_copy(j).wait_send())
 
     @pl.when(jnp.logical_and(jnp.logical_not(last), jnp.logical_not(first)))
     def _():
         each(chunks, lambda j: c2_copy(j).wait_send())
+
+    @pl.when(relay)
+    def _():
+        each(pairs - DIRECT, lambda p: warm_back(p + DIRECT).wait_send())
 
     each(chunks, lambda j: out_copy(j, e2).wait())
     for i in range(ITERS):
@@ -332,17 +407,20 @@
         out_specs=(any_, pl.BlockSpec(memory_space=pltpu.SMEM)),
         scratch_shapes=[
             pltpu.VMEM((layers, blocks, picks * size, size), jnp.bfloat16),
-            *[pltpu.VMEM(piece, jnp.bfloat16)] * 6,
+            *[pltpu.VMEM(piece, jnp.bfloat16)] * 7,
             pltpu.VMEM(piece, jnp.float32),
             pltpu.VMEM((blocks, ROWS, size), jnp.bfloat16),
             *[pltpu.VMEM((blocks, PAIR * ROWS, size), jnp.bfloat16)] * 2,
             *[pltpu.VMEM((blocks, PAIR * ROWS, size), jnp.float32)] * 3,
+            *[pltpu.VMEM((blocks, QUAD * ROWS, size), jnp.bfloat16)] * 2,
+            pltpu.VMEM((blocks, QUAD * ROWS, size), jnp.float32),
             pltpu.VMEM((3, 8, BLOCK), jnp.float32),
             *[pltpu.VMEM((ITERS, 8, BLOCK), jnp.float32)] * 2,
             pltpu.VMEM((peers - 1, ITERS, 8, BLOCK), jnp.float32),
             pltpu.VMEM((ITERS, 8, BLOCK), jnp.float32),
             dma((layers,)),
-            *[dma((chunks,))] * 8,
+            *[dma((chunks // PAIR,))] * 5,
+            *[dma((chunks,))] * 5,
             dma, dma, dma((peers - 1,)), dma((peers - 1,)), dma((chain - 1,)), dma,
         ],
         compiler_params=pltpu.CompilerParams(

time: 165 us -> 148 us (0.90)
  Pallas kernels: 161 us -> 143 us
    pallas_call x1, Pallas kernels: 161 us -> 143 us  [on_device(): pl.pallas_call(functools.partial(kernel, chain, peers), out_shape=(jax.Sh...]
where the time goes in v3:
time: 148 us; the launch traced here: 147 us
  Pallas kernels  143 us (97%)
  local copies, waits for them, and re-layouts  2.29 us (2%)
    pallas_call x1, Pallas kernels, on_device(): pl.pallas_call(functools.partial(kernel, chain, peers), out_shape=(jax.Sh...  143 us

profile of v3, /device:TPU:0, one launch (start us, length us, event | category | flops | bytes accessed | tf_op | source)
XLA Modules:
  0.0 147.3 jit_solution(16516497546516619054)
XLA Ops:
  0.6 143.2 %shard_map.68 = (bf16[16,32,8,128]{3,2,1,0:T(8,128)(2,1)}, f32[2]{0:T(128)}) custom-call(s32[4,4,32]{2,1,0:T(4,128)} %bitcast.15, bf16[16,32,8,128]{3,2,1,0:T(8,128)(2,1)} %bitcast.12, bf16[16,32,8,128]{3,2,1,0:T(8,128)(2,1)} %bitcast.13, bf16[4,32,512,128]{3,2,1,0:T(8,128)(2,1)} %bitcast.11, f32[4,4096]{1,0:T(4,128)} %bias.1), custom_call_target="tpu_custom_call" | custom-call | tf_op jit(solution)/shard_map/pallas_call | solution.py:400
  143.9 1.1 multiply_sqrt_fusion
  145.0 2.3 %copy.8 = bf16[1,128,4096]{2,1,0:T(8,128)(2,1)} copy(bf16[1,128,4096]{2,1,0:T(8,128)(2,1)} %bitcast.14) | data formatting | bytes 2097152

commit v4 on v3

--- a/solution.py
+++ b/solution.py
@@ -13,13 +13,14 @@
 ROWS = 8
 PAIR = 2
 QUAD = 4
+CUT = 2
 DIRECT = 2
 SIDE = 4
 BLOCK = 128
 
 
 def kernel(chain, peers, pat, inputs, warm, weights, bias, out, norms, w, start, own, c1, c2, e1, e2, hold, tau,
-           xs, xa, xb, gc, ref, comb, ya, yb, gy, acc, part, before, around, total, w_sem, own_sem, start_send, start_recv,
+           xs, ya, yb, gc, ref, comb, acc, part, before, around, total, w_sem, own_sem, start_send, start_recv,
            hold_send, hold_recv, c1_send, c1_recv,
            c2_send, c2_recv, out_sem,
            part_send, part_recv, peer_send, peer_recv, total_send, total_recv):
@@ -31,6 +32,7 @@
     chunks = inputs.shape[0]
     pairs = chunks // PAIR
     first, second, last = me == 0, me == 1, me == chain - 1
+    quads = chunks // QUAD
     sender = me < SIDE
     aside = jnp.where(me < SIDE - 1, chain - SIDE + 1 + me, 0)
     late = me > chain - SIDE
@@ -67,11 +69,20 @@
             src_ref=pair(hold, p), dst_ref=pair(start, p), send_sem=hold_send.at[p],
             recv_sem=start_recv.at[p], device_id={"layer": target}, device_id_type=MESH)
 
-    def c1_copy(j):
-        return to_next(e1.at[j], c1.at[j], c1_send.at[j], c1_recv.at[j])
-
-    def c2_copy(j):
-        return to_next(e2.at[j], c2.at[j], c2_send.at[j], c2_recv.at[j])
+    def slab(ref, j, h):
+        return ref.at[j, pl.ds(h * (blocks // CUT), blocks // CUT)]
+
+    def c1_copy(j, h, src=e1):
+        at = j * CUT + h
+        return to_next(slab(src, j, h), slab(c1, j, h), c1_send.at[at], c1_recv.at[at])
+
+    def c2_copy(j, h):
+        at = j * CUT + h
+        return to_next(slab(e2, j, h), slab(c2, j, h), c2_send.at[at], c2_recv.at[at])
+
+    def halves(do):
+        for h in range(CUT):
+            do(h)
 
     def part_copy():
         return to_next(part, before, part_send, part_recv)
@@ -96,15 +107,18 @@
             return carry
         lax.fori_loop(0, count, body, 0)
 
+    def fetch(lo, hi):
+        @pl.when(first)
+        def _():
+            each(hi - lo, lambda p: input_copy(p + lo).start())
+
+        each(hi - lo, lambda p: own_copy(p + lo).start())
+
     weight_copy(0).start()
-
-    @pl.when(first)
-    def _():
-        each(pairs, lambda p: input_copy(p).start())
-
-    each(pairs, lambda p: own_copy(p).start())
+    fetch(0, DIRECT)
     for layer in range(1, layers):
         weight_copy(layer).start()
+    fetch(DIRECT, pairs)
 
     barrier = pltpu.get_barrier_semaphore()
 
@@ -161,25 +175,17 @@
 
     acc[...] = jnp.zeros_like(acc)
 
-    def layer_of(layer, src, epilogue, unroll=True):
+    def layer_of(layer, src, epilogue, lo=0, hi=blocks, unroll=True):
         def body(c, carry):
             taken = [src[pat[layer, k, c]] for k in range(picks)]
             pre = jnp.dot(jnp.concatenate(taken, axis=1), w[layer, c],
                           preferred_element_type=jnp.float32)
             epilogue(c, jnp.tanh(pre + bias[layer:layer + 1, pl.ds(c * BLOCK, BLOCK)]))
             return carry
-        lax.fori_loop(0, blocks, body, 0, unroll=unroll)
+        lax.fori_loop(lo, hi, body, 0, unroll=unroll)
 
     def fold(x):
         return jnp.sum(x.reshape(x.shape[0] // 8, 8, BLOCK), axis=0)
-
-    def fine(src, dst, final):
-        for layer in range(1, layers - 1):
-            def middle(c, t, src=src, dst=dst):
-                dst[c] = (src[c].astype(jnp.float32) + STEP * t).astype(jnp.bfloat16)
-            layer_of(layer, src, middle)
-            src, dst = dst, src
-        layer_of(layers - 1, src, lambda c, t: final(c, src, t))
 
     def relax_first(q):
         for i in range(QUAD // PAIR):
@@ -196,108 +202,101 @@
             own_copy(p).wait()
         x = [start[q * QUAD + i].astype(jnp.float32) for i in range(QUAD)]
         ya[...] = jnp.concatenate(x, axis=1).astype(jnp.bfloat16)
+        for i in range(QUAD):
+            ref[:, i * ROWS:(i + 1) * ROWS] = own[q * QUAD + i].astype(jnp.float32)
+
+        @pl.when(q == 0)
+        def _():
+            weight_copy(0).wait()
 
         def entry(c, t):
             x = ya[c].astype(jnp.float32)
-            gy[c] = x + factor * t
+            gc[c] = x + factor * t
             yb[c] = (x + STEP * t).astype(jnp.bfloat16)
-        layer_of(0, ya, entry, 16)
-
-        def final(c, src, t):
-            g = (src[c].astype(jnp.float32) + STEP * t).astype(jnp.bfloat16).astype(jnp.float32)
-            coarse = gy[c]
-            correction = g - coarse
-            joined = (coarse + correction).astype(jnp.bfloat16)
-            for i in range(QUAD):
-                j = q * QUAD + i
-                at_rows = slice(i * ROWS, (i + 1) * ROWS)
-                tau[j, c] = correction[at_rows]
-                e1[j, c] = joined[at_rows]
-                off = g[at_rows] - own[j, c].astype(jnp.float32)
-                acc[0] += off * off
-            off = g - joined.astype(jnp.float32)
-            acc[2] += fold(off * off)
-        fine(yb, ya, final)
-
-    def sweep_first(p):
+        layer_of(0, ya, entry, unroll=16)
+
+    def sweeps(q):
         def chunk(i, carry):
-            j = p * PAIR + i
-            c1_copy(j).wait_recv()
-            xs[...] = c1[j]
-            at_rows = pl.ds(pl.multiple_of(i * ROWS, ROWS), ROWS)
-
-            def epilogue(c, t):
-                x = xs[c].astype(jnp.float32)
-                coarse = x + factor * t
-                end = (coarse + tau[j, c]).astype(jnp.bfloat16)
-                e1[j, c] = end
-                gc[c, at_rows] = coarse
-                ref[c, at_rows] = end.astype(jnp.float32)
-                comb[c, at_rows] = x + STEP * t
-            layer_of(0, xs, epilogue)
+            @pl.when(jnp.logical_and(q > 0, jnp.logical_not(second)))
+            def _():
+                sweep_second((q - 1) * QUAD + i)
+
+            @pl.when(q < quads)
+            def _():
+                sweep_first(q * QUAD + i, i)
+            return carry
+        lax.fori_loop(0, QUAD, chunk, 0)
+        yb[...] = comb[...].astype(jnp.bfloat16)
+
+    def sweep_first(j, i):
+        halves(lambda h: c1_copy(j, h).wait_recv())
+        xs[...] = c1[j]
+        at_rows = pl.ds(pl.multiple_of(i * ROWS, ROWS), ROWS)
+
+        def epilogue(c, t):
+            x = xs[c].astype(jnp.float32)
+            coarse = x + factor * t
+            end = (coarse + tau[j, c]).astype(jnp.bfloat16)
+            e1[j, c] = end
+            gc[c, at_rows] = coarse
+            ref[c, at_rows] = end.astype(jnp.float32)
+            comb[c, at_rows] = x + STEP * t
+
+        def part_of(h):
+            layer_of(0, xs, epilogue, h * (blocks // CUT), (h + 1) * (blocks // CUT))
 
             @pl.when(jnp.logical_not(last))
             def _():
-                c1_copy(j).start()
-            return carry
-        lax.fori_loop(0, PAIR, chunk, 0)
-        xb[...] = comb[...].astype(jnp.bfloat16)
-
-        def final(c, src, t):
-            g = (src[c].astype(jnp.float32) + STEP * t).astype(jnp.bfloat16).astype(jnp.float32)
-            coarse = gc[c]
-            correction = g - coarse
-            joined = (coarse + correction).astype(jnp.bfloat16)
-            for i in range(PAIR):
-                j = p * PAIR + i
-                at_rows = slice(i * ROWS, (i + 1) * ROWS)
-                tau[j, c] = correction[at_rows]
-                e2[j, c] = joined[at_rows]
-            off = g - ref[c]
-            acc[1] += fold(off * off)
-        fine(xb, xa, final)
-
-    def sweep_second(p):
-        def chunk(i, carry):
-            j = p * PAIR + i
-            c2_copy(j).wait_recv()
-            xs[...] = c2[j]
-
-            def epilogue(c, t):
-                x = xs[c].astype(jnp.float32)
-                e2[j, c] = (x + factor * t + tau[j, c]).astype(jnp.bfloat16)
-            layer_of(0, xs, epilogue)
+                c1_copy(j, h).start()
+        halves(part_of)
+
+    def fine(q, phase):
+        src, dst = yb, ya
+        for layer in range(1, layers):
+            @pl.when(jnp.logical_and(q == 0, phase == 0))
+            def _(layer=layer):
+                weight_copy(layer).wait()
+
+            def middle(c, t, src=src, dst=dst):
+                dst[c] = (src[c].astype(jnp.float32) + STEP * t).astype(jnp.bfloat16)
+
+            def final(c, t, src=src):
+                g = (src[c].astype(jnp.float32) + STEP * t).astype(jnp.bfloat16).astype(jnp.float32)
+                coarse = gc[c]
+                correction = g - coarse
+                joined = (coarse + correction).astype(jnp.bfloat16)
+                for i in range(QUAD):
+                    j = q * QUAD + i
+                    at_rows = slice(i * ROWS, (i + 1) * ROWS)
+                    tau[j, c] = correction[at_rows]
+                    e2[j, c] = joined[at_rows]
+                off = g - ref[c]
+                acc[phase] += fold(off * off)
+                off = g - joined.astype(jnp.float32)
+                acc[2] += fold(off * off)
+            layer_of(layer, src, middle if layer < layers - 1 else final)
+            src, dst = dst, src
+
+    def sweep_second(j):
+        halves(lambda h: c2_copy(j, h).wait_recv())
+        xs[...] = c2[j]
+
+        def epilogue(c, t):
+            x = xs[c].astype(jnp.float32)
+            e2[j, c] = (x + factor * t + tau[j, c]).astype(jnp.bfloat16)
+
+        def part_of(h):
+            layer_of(0, xs, epilogue, h * (blocks // CUT), (h + 1) * (blocks // CUT))
 
             @pl.when(jnp.logical_not(last))
             def _():
-                c2_copy(j).start()
-            out_copy(j, e2).start()
-            return carry
-        lax.fori_loop(0, PAIR, chunk, 0)
-
-    for layer in range(layers):
-        weight_copy(layer).wait()
-
-    quads = chunks // QUAD
-    lead = jnp.where(first, quads, jnp.clip(2 * (me - SIDE) + 1, 0, quads))
-
-    def sweeps(p, carry):
-        sweep_first(p)
-
-        @pl.when(p == pairs - 1)
-        def _():
-            gather_part()
-
-        @pl.when(second)
-        def _():
-            for i in range(PAIR):
-                c2_copy(p * PAIR + i).start()
-                out_copy(p * PAIR + i, e2).start()
-
-        @pl.when(jnp.logical_not(second))
-        def _():
-            sweep_second(p)
-        return carry
+                c2_copy(j, h).start()
+        halves(part_of)
+        out_copy(j, e2).start()
+
+        @pl.when(jnp.logical_and(last, j == chunks - 3))
+        def _():
+            spread_total()
 
     def gather_part():
         part[0] = acc[0]
@@ -317,48 +316,71 @@
             for hop in range(1, peers):
                 peer_copy(hop).start()
 
-    def step(s, carry):
-        @pl.when(s < quads)
-        def _():
-            relax_first(s)
-
-            @pl.when(first)
-            def _():
-                for i in range(QUAD):
-                    c1_copy(s * QUAD + i).start()
-                    out_copy(s * QUAD + i, e1).start()
-                for i in range(QUAD // PAIR):
-                    p = s * (QUAD // PAIR) + i
-
-                    @pl.when(p >= DIRECT)
-                    def _():
-                        pass_on(p)
-
-        @pl.when(jnp.logical_and(s == quads - 1, me == chain - SIDE))
-        def _():
-            each(pairs, lambda p: warm_send(p).start())
-
-        @pl.when(jnp.logical_and(s >= lead, jnp.logical_not(first)))
-        def _():
-            q = s - lead
-            lax.fori_loop(q * (QUAD // PAIR), (q + 1) * (QUAD // PAIR), sweeps, 0)
-
-        return carry
-
-    lax.fori_loop(0, jnp.where(first, quads, quads + lead), step, 0)
-
-    @pl.when(first)
-    def _():
-        gather_part()
-
-    @pl.when(last)
-    def _():
+    def spread_total():
         for hop in range(1, peers):
             peer_copy(hop).wait()
         part[...] += jnp.sum(around[...], axis=0)
         for layer in range(chain - 1):
             total_copy(layer).start()
         total[...] = part[...]
+
+    lead = jnp.where(first, 0, jnp.clip(2 * (me - SIDE) + 1, 0, quads))
+
+    def step(s, carry):
+        def phase_of(phase, carry):
+            q = jnp.where(phase == 0, s, s - lead)
+            run = jnp.where(phase == 0, s < quads,
+                            jnp.logical_and(q >= 0, jnp.logical_not(first)))
+
+            @pl.when(run)
+            def _():
+                @pl.when(phase == 0)
+                def _():
+                    relax_first(q)
+
+                @pl.when(phase == 1)
+                def _():
+                    sweeps(q)
+
+                @pl.when(q < quads)
+                def _():
+                    fine(q, phase)
+            return carry
+        lax.fori_loop(0, ITERS, phase_of, 0)
+        q = s - lead
+
+        @pl.when(q == quads - 1)
+        def _():
+            gather_part()
+
+        @pl.when(first)
+        def _():
+            for i in range(QUAD):
+                halves(lambda h: c1_copy(q * QUAD + i, h, e2).start())
+                out_copy(q * QUAD + i, e2).start()
+            for i in range(QUAD // PAIR):
+                p = q * (QUAD // PAIR) + i
+
+                @pl.when(p >= DIRECT)
+                def _():
+                    pass_on(p)
+
+        @pl.when(second)
+        def _():
+            for i in range(QUAD):
+                halves(lambda h: c2_copy(q * QUAD + i, h).start())
+                out_copy(q * QUAD + i, e2).start()
+
+        @pl.when(jnp.logical_and(s == quads - 1, me == chain - SIDE))
+        def _():
+            each(pairs, lambda p: warm_send(p).start())
+
+        return carry
+
+    lax.fori_loop(0, quads + lead + jnp.where(me >= 2, 1, 0), step, 0)
+
+    @pl.when(last)
+    def _():
         for layer in range(chain - 1):
             total_copy(layer).wait_send()
 
@@ -367,11 +389,11 @@
         part_copy().wait_send()
         total_copy(0).wait_recv()
         each(pairs, lambda p: warm_send(p).wait_send())
-        each(chunks, lambda j: c1_copy(j).wait_send())
+        each(chunks, lambda j: halves(lambda h: c1_copy(j, h).wait_send()))
 
     @pl.when(jnp.logical_and(jnp.logical_not(last), jnp.logical_not(first)))
     def _():
-        each(chunks, lambda j: c2_copy(j).wait_send())
+        each(chunks, lambda j: halves(lambda h: c2_copy(j, h).wait_send()))
 
     @pl.when(relay)
     def _():
@@ -410,17 +432,16 @@
             *[pltpu.VMEM(piece, jnp.bfloat16)] * 7,
             pltpu.VMEM(piece, jnp.float32),
             pltpu.VMEM((blocks, ROWS, size), jnp.bfloat16),
-            *[pltpu.VMEM((blocks, PAIR * ROWS, size), jnp.bfloat16)] * 2,
-            *[pltpu.VMEM((blocks, PAIR * ROWS, size), jnp.float32)] * 3,
             *[pltpu.VMEM((blocks, QUAD * ROWS, size), jnp.bfloat16)] * 2,
-            pltpu.VMEM((blocks, QUAD * ROWS, size), jnp.float32),
+            *[pltpu.VMEM((blocks, QUAD * ROWS, size), jnp.float32)] * 3,
             pltpu.VMEM((3, 8, BLOCK), jnp.float32),
             *[pltpu.VMEM((ITERS, 8, BLOCK), jnp.float32)] * 2,
             pltpu.VMEM((peers - 1, ITERS, 8, BLOCK), jnp.float32),
             pltpu.VMEM((ITERS, 8, BLOCK), jnp.float32),
             dma((layers,)),
             *[dma((chunks // PAIR,))] * 5,
-            *[dma((chunks,))] * 5,
+            *[dma((chunks * CUT,))] * 4,
+            dma((chunks,)),
             dma, dma, dma((peers - 1,)), dma((peers - 1,)), dma((chain - 1,)), dma,
         ],
         compiler_params=pltpu.CompilerParams(

time: 148 us -> 141 us (0.953)
  Pallas kernels: 143 us -> 136 us
    pallas_call x1, Pallas kernels: 143 us -> 136 us  [on_device(): pl.pallas_call(functools.partial(kernel, chain, peers), out_shape=(jax.Sh...]
where the time goes in v4:
time: 141 us
  Pallas kernels  136 us (96%)
  local copies, waits for them, and re-layouts  2.29 us (2%)
    pallas_call x1, Pallas kernels, on_device(): pl.pallas_call(functools.partial(kernel, chain, peers), out_shape=(jax.Sh...  136 us

profile of v4, /device:TPU:0, one launch (start us, length us, event | category | flops | bytes accessed | tf_op | source)
XLA Modules:
  0.0 140.5 jit_solution(7171442141816699967)
XLA Ops:
  0.6 136.5 %shard_map.68 = (bf16[16,32,8,128]{3,2,1,0:T(8,128)(2,1)}, f32[2]{0:T(128)}) custom-call(s32[4,4,32]{2,1,0:T(4,128)} %bitcast.15, bf16[16,32,8,128]{3,2,1,0:T(8,128)(2,1)} %bitcast.12, bf16[16,32,8,128]{3,2,1,0:T(8,128)(2,1)} %bitcast.13, bf16[4,32,512,128]{3,2,1,0:T(8,128)(2,1)} %bitcast.11, f32[4,4096]{1,0:T(4,128)} %bias.1), custom_call_target="tpu_custom_call" | custom-call | tf_op jit(solution)/shard_map/pallas_call | solution.py:422
  137.1 1.1 multiply_sqrt_fusion
  138.2 2.3 %copy.8 = bf16[1,128,4096]{2,1,0:T(8,128)(2,1)} copy(bf16[1,128,4096]{2,1,0:T(8,128)(2,1)} %bitcast.14) | data formatting | bytes 2097152

commit v5 on v4

--- a/solution.py
+++ b/solution.py
@@ -15,12 +15,13 @@
 QUAD = 4
 CUT = 2
 DIRECT = 2
+SPREAD = 8
 SIDE = 4
 BLOCK = 128
 
 
 def kernel(chain, peers, pat, inputs, warm, weights, bias, out, norms, w, start, own, c1, c2, e1, e2, hold, tau,
-           xs, ya, yb, gc, ref, comb, acc, part, before, around, total, w_sem, own_sem, start_send, start_recv,
+           xs, ya, yb, gy, za, zb, gc, ref, comb, acc, part, before, around, total, w_sem, own_sem, start_send, start_recv,
            hold_send, hold_recv, c1_send, c1_recv,
            c2_send, c2_recv, out_sem,
            part_send, part_recv, peer_send, peer_recv, total_send, total_recv):
@@ -202,36 +203,37 @@
             own_copy(p).wait()
         x = [start[q * QUAD + i].astype(jnp.float32) for i in range(QUAD)]
         ya[...] = jnp.concatenate(x, axis=1).astype(jnp.bfloat16)
-        for i in range(QUAD):
-            ref[:, i * ROWS:(i + 1) * ROWS] = own[q * QUAD + i].astype(jnp.float32)
-
         @pl.when(q == 0)
         def _():
             weight_copy(0).wait()
 
         def entry(c, t):
             x = ya[c].astype(jnp.float32)
-            gc[c] = x + factor * t
+            gy[c] = x + factor * t
             yb[c] = (x + STEP * t).astype(jnp.bfloat16)
         layer_of(0, ya, entry, unroll=16)
 
-    def sweeps(q):
+        def off_of(g, c, i):
+            return g - own[q * QUAD + i, c].astype(jnp.float32)
+        fine(yb, ya, gy, off_of, q * QUAD, QUAD, 0, q == 0)
+
+    def sweep_ahead(q):
         def chunk(i, carry):
-            @pl.when(jnp.logical_and(q > 0, jnp.logical_not(second)))
-            def _():
-                sweep_second((q - 1) * QUAD + i)
-
-            @pl.when(q < quads)
-            def _():
-                sweep_first(q * QUAD + i, i)
+            sweep_first(q * QUAD + i)
             return carry
         lax.fori_loop(0, QUAD, chunk, 0)
-        yb[...] = comb[...].astype(jnp.bfloat16)
-
-    def sweep_first(j, i):
+
+    def relax_second():
+        zb[...] = comb[...].astype(jnp.bfloat16)
+
+        def off_of(g, c, i):
+            return g - ref[c, i * ROWS:(i + 1) * ROWS]
+        fine(zb, za, gc, off_of, 0, chunks, 1)
+
+    def sweep_first(j):
         halves(lambda h: c1_copy(j, h).wait_recv())
         xs[...] = c1[j]
-        at_rows = pl.ds(pl.multiple_of(i * ROWS, ROWS), ROWS)
+        at_rows = pl.ds(pl.multiple_of(j * ROWS, ROWS), ROWS)
 
         def epilogue(c, t):
             x = xs[c].astype(jnp.float32)
@@ -250,30 +252,32 @@
                 c1_copy(j, h).start()
         halves(part_of)
 
-    def fine(q, phase):
-        src, dst = yb, ya
+    def fine(src, dst, base, off_of, start_at, count, phase, fresh=None):
         for layer in range(1, layers):
-            @pl.when(jnp.logical_and(q == 0, phase == 0))
-            def _(layer=layer):
-                weight_copy(layer).wait()
+            if fresh is not None:
+                @pl.when(fresh)
+                def _(layer=layer):
+                    weight_copy(layer).wait()
 
             def middle(c, t, src=src, dst=dst):
                 dst[c] = (src[c].astype(jnp.float32) + STEP * t).astype(jnp.bfloat16)
 
             def final(c, t, src=src):
                 g = (src[c].astype(jnp.float32) + STEP * t).astype(jnp.bfloat16).astype(jnp.float32)
-                coarse = gc[c]
+                coarse = base[c]
                 correction = g - coarse
                 joined = (coarse + correction).astype(jnp.bfloat16)
-                for i in range(QUAD):
-                    j = q * QUAD + i
+                total_off = jnp.zeros((ROWS, BLOCK), jnp.float32)
+                for i in range(count):
                     at_rows = slice(i * ROWS, (i + 1) * ROWS)
-                    tau[j, c] = correction[at_rows]
-                    e2[j, c] = joined[at_rows]
-                off = g - ref[c]
-                acc[phase] += fold(off * off)
-                off = g - joined.astype(jnp.float32)
-                acc[2] += fold(off * off)
+                    tau[start_at + i, c] = correction[at_rows]
+                    e2[start_at + i, c] = joined[at_rows]
+                    off = off_of(g[at_rows], c, i)
+                    total_off += off * off
+                acc[phase] += total_off
+                if phase == 0:
+                    off = g - joined.astype(jnp.float32)
+                    acc[2] += fold(off * off)
             layer_of(layer, src, middle if layer < layers - 1 else final)
             src, dst = dst, src
 
@@ -294,7 +298,11 @@
         halves(part_of)
         out_copy(j, e2).start()
 
-        @pl.when(jnp.logical_and(last, j == chunks - 3))
+        @pl.when(j == 1)
+        def _():
+            gather_part()
+
+        @pl.when(jnp.logical_and(last, j == SPREAD))
         def _():
             spread_total()
 
@@ -327,31 +335,11 @@
     lead = jnp.where(first, 0, jnp.clip(2 * (me - SIDE) + 1, 0, quads))
 
     def step(s, carry):
-        def phase_of(phase, carry):
-            q = jnp.where(phase == 0, s, s - lead)
-            run = jnp.where(phase == 0, s < quads,
-                            jnp.logical_and(q >= 0, jnp.logical_not(first)))
-
-            @pl.when(run)
-            def _():
-                @pl.when(phase == 0)
-                def _():
-                    relax_first(q)
-
-                @pl.when(phase == 1)
-                def _():
-                    sweeps(q)
-
-                @pl.when(q < quads)
-                def _():
-                    fine(q, phase)
-            return carry
-        lax.fori_loop(0, ITERS, phase_of, 0)
         q = s - lead
 
-        @pl.when(q == quads - 1)
-        def _():
-            gather_part()
+        @pl.when(s < quads)
+        def _():
+            relax_first(s)
 
         @pl.when(first)
         def _():
@@ -365,19 +353,36 @@
                 def _():
                     pass_on(p)
 
-        @pl.when(second)
-        def _():
-            for i in range(QUAD):
-                halves(lambda h: c2_copy(q * QUAD + i, h).start())
-                out_copy(q * QUAD + i, e2).start()
-
         @pl.when(jnp.logical_and(s == quads - 1, me == chain - SIDE))
         def _():
             each(pairs, lambda p: warm_send(p).start())
 
+        @pl.when(jnp.logical_and(q >= 0, jnp.logical_not(first)))
+        def _():
+            sweep_ahead(q)
+
         return carry
 
-    lax.fori_loop(0, quads + lead + jnp.where(me >= 2, 1, 0), step, 0)
+    lax.fori_loop(0, quads + lead, step, 0)
+
+    @pl.when(jnp.logical_not(first))
+    def _():
+        relax_second()
+
+    @pl.when(me < 2)
+    def _():
+        gather_part()
+
+    @pl.when(second)
+    def _():
+        def send(j):
+            halves(lambda h: c2_copy(j, h).start())
+            out_copy(j, e2).start()
+        each(chunks, send)
+
+    @pl.when(me >= 2)
+    def _():
+        each(chunks, sweep_second)
 
     @pl.when(last)
     def _():
@@ -433,7 +438,9 @@
             pltpu.VMEM(piece, jnp.float32),
             pltpu.VMEM((blocks, ROWS, size), jnp.bfloat16),
             *[pltpu.VMEM((blocks, QUAD * ROWS, size), jnp.bfloat16)] * 2,
-            *[pltpu.VMEM((blocks, QUAD * ROWS, size), jnp.float32)] * 3,
+            pltpu.VMEM((blocks, QUAD * ROWS, size), jnp.float32),
+            *[pltpu.VMEM((blocks, rows, size), jnp.bfloat16)] * 2,
+            *[pltpu.VMEM((blocks, rows, size), jnp.float32)] * 3,
             pltpu.VMEM((3, 8, BLOCK), jnp.float32),
             *[pltpu.VMEM((ITERS, 8, BLOCK), jnp.float32)] * 2,
             pltpu.VMEM((peers - 1, ITERS, 8, BLOCK), jnp.float32),

time: 141 us -> 128 us (0.908)
  Pallas kernels: 136 us -> 124 us
    pallas_call x1, Pallas kernels: 136 us -> 124 us  [on_device(): pl.pallas_call(functools.partial(kernel, chain, peers), out_shape=(jax.Sh...]
where the time goes in v5:
time: 128 us
  Pallas kernels  124 us (97%)
  local copies, waits for them, and re-layouts  2.29 us (2%)
    pallas_call x1, Pallas kernels, on_device(): pl.pallas_call(functools.partial(kernel, chain, peers), out_shape=(jax.Sh...  124 us

profile of v5, /device:TPU:0, one launch (start us, length us, event | category | flops | bytes accessed | tf_op | source)
XLA Modules:
  0.0 128.2 jit_solution(908236291437128840)
XLA Ops:
  0.6 124.2 %shard_map.68 = (bf16[16,32,8,128]{3,2,1,0:T(8,128)(2,1)}, f32[2]{0:T(128)}) custom-call(s32[4,4,32]{2,1,0:T(4,128)} %bitcast.15, bf16[16,32,8,128]{3,2,1,0:T(8,128)(2,1)} %bitcast.12, bf16[16,32,8,128]{3,2,1,0:T(8,128)(2,1)} %bitcast.13, bf16[4,32,512,128]{3,2,1,0:T(8,128)(2,1)} %bitcast.11, f32[4,4096]{1,0:T(4,128)} %bias.1), custom_call_target="tpu_custom_call" | custom-call | tf_op jit(solution)/shard_map/pallas_call | solution.py:427
  124.8 1.1 multiply_sqrt_fusion
  125.9 2.3 %copy.8 = bf16[1,128,4096]{2,1,0:T(8,128)(2,1)} copy(bf16[1,128,4096]{2,1,0:T(8,128)(2,1)} %bitcast.14) | data formatting | bytes 2097152

commit v6 on v5

--- a/solution.py
+++ b/solution.py
@@ -15,7 +15,7 @@
 QUAD = 4
 CUT = 2
 DIRECT = 2
-SPREAD = 8
+SPREAD = 6
 SIDE = 4
 BLOCK = 128
 

time: 128 us -> 126 us (0.984)
  Pallas kernels: 124 us -> 122 us
    pallas_call x1, Pallas kernels: 124 us -> 122 us  [on_device(): pl.pallas_call(functools.partial(kernel, chain, peers), out_shape=(jax.Sh...]
where the time goes in v6:
time: 126 us
  Pallas kernels  122 us (97%)
  local copies, waits for them, and re-layouts  2.29 us (2%)
    pallas_call x1, Pallas kernels, on_device(): pl.pallas_call(functools.partial(kernel, chain, peers), out_shape=(jax.Sh...  122 us

profile of v6, /device:TPU:0, one launch (start us, length us, event | category | flops | bytes accessed | tf_op | source)
XLA Modules:
  0.0 126.0 jit_solution(12845385853142543575)
XLA Ops:
  0.6 122.0 %shard_map.68 = (bf16[16,32,8,128]{3,2,1,0:T(8,128)(2,1)}, f32[2]{0:T(128)}) custom-call(s32[4,4,32]{2,1,0:T(4,128)} %bitcast.15, bf16[16,32,8,128]{3,2,1,0:T(8,128)(2,1)} %bitcast.12, bf16[16,32,8,128]{3,2,1,0:T(8,128)(2,1)} %bitcast.13, bf16[4,32,512,128]{3,2,1,0:T(8,128)(2,1)} %bitcast.11, f32[4,4096]{1,0:T(4,128)} %bias.1), custom_call_target="tpu_custom_call" | custom-call | tf_op jit(solution)/shard_map/pallas_call | solution.py:427
  122.6 1.1 multiply_sqrt_fusion
  123.7 2.3 %copy.8 = bf16[1,128,4096]{2,1,0:T(8,128)(2,1)} copy(bf16[1,128,4096]{2,1,0:T(8,128)(2,1)} %bitcast.14) | data formatting | bytes 2097152
